TPU v7x, 32 devices: a whole 2x2x4 slice. The times are simulated.
32 devices in a mesh: dp: 8 (over z, y), row: 2 (over core), col: 2 (over x).
Axes of the slice: x: 2, y: 2, z: 4, core: 2. Of those that a mesh axis runs over, the one named last changes fastest.
Arguments:
- inputs: bfloat16 [4096, 2048], P(('dp', 'row'), 'col'), may hold values from -6 to 6
- gain_attn: float32 [2048], P('col'), may hold values from 0.5 to 1.5
- w_keys: bfloat16 [2048, 4096], P('col', 'row'), may hold values from -0.125 to 0.125
- w_values: bfloat16 [2048, 8224], P('col', 'row'), may hold values from -0.125 to 0.125
- conv_weight: float32 [4, 8192], P(None, 'row'), may hold values from -3 to 3
- decay_log: float32 [16], P('row'), may hold values from -4 to 0.5
- step_bias: float32 [16], P('row'), may hold values from -2 to 1
- gain_head: float32 [256], replicated, may hold values from 0.5 to 1.5
- w_out: bfloat16 [4096, 2048], P('row', 'col'), may hold values from -0.1875 to 0.1875
- gain_mlp: float32 [2048], P('col'), may hold values from 0.5 to 1.5
- w_gate: bfloat16 [2048, 5504], P('col', 'row'), may hold values from -0.125 to 0.125
- w_up: bfloat16 [2048, 5504], P('col', 'row'), may hold values from -0.125 to 0.125
- w_down: bfloat16 [5504, 2048], P('row', 'col'), may hold values from -0.109375 to 0.109375
- seq_lens: int32 [16, 3], P('dp'), may hold values from 1 to 128, 256 in all within a row
- cotangent: float32 [4096, 2048], P(('dp', 'row'), 'col'), may hold values from -6 to 6
Outputs:
- result: float32 [4096, 2048], P(('dp', 'row'), 'col')
- input_grad: float32 [4096, 2048], P(('dp', 'row'), 'col')
- grad_gain_attn: float32 [2048], P('col')
- grad_w_keys: float32 [2048, 4096], P('col', 'row')
- grad_w_values: float32 [2048, 8224], P('col', 'row')
- grad_conv: float32 [4, 8192], P(None, 'row')
- grad_decay_log: float32 [16], P('row')
- grad_step_bias: float32 [16], P('row')
- grad_gain_head: float32 [256], replicated
- grad_w_out: float32 [4096, 2048], P('row', 'col')
- grad_gain_mlp: float32 [2048], P('col')
- grad_w_gate: float32 [2048, 5504], P('col', 'row')
- grad_w_up: float32 [2048, 5504], P('col', 'row')
- grad_w_down: float32 [5504, 2048], P('row', 'col')
Inputs may be any that keep to these rules, and one draw needn't show every extreme that they name: `seq_lens`: row b describes packed block b, the token rows b * 256 to (b + 1) * 256 - 1: the lengths of two documents placed in order from the block's start, then the number of padded slots after them; each row sums to 256, and its largest entry is 128.
All inputs are finite; a program needn't handle non-finite values.
Results may differ from a plain program's by a relative error of at most 0.015.
Values may be sent and summed in bfloat16 or wider, within the bound.
A program may use at most 320 MiB of HBM per device.

v0:
```python
from functools import partial

import jax
import jax.numpy as jnp
from jax import lax
from jax.sharding import PartitionSpec as P

D = 2048
DK = 128
DV = 256
KCONV = 4
BLOCK = 64


exact_setting = lax.Precision.HIGHEST


def to_blocks(tensor, blocks):
    shaped = tensor.reshape((blocks, BLOCK) + tensor.shape[1:])
    return jnp.swapaxes(shaped, 1, 2)


def delta_mixer(keys_proj, values_proj, conv_weight, decay_log, step_bias, gain_head, segment):
    length = keys_proj.shape[0]
    head_count = keys_proj.shape[1] // (2 * DK)
    key_part = keys_proj.reshape(length, head_count, 2 * DK)
    value_part = values_proj.reshape(length, head_count, 2 * DV + 2)
    conv_in = jnp.concatenate([key_part, value_part[:, :, :DV]], axis=2).reshape(
        length, head_count * (2 * DK + DV)
    )
    conv_sum = conv_weight[0][None, :] * conv_in
    for offset in range(1, KCONV):
        earlier = jnp.concatenate(
            [jnp.zeros((offset, conv_in.shape[1]), jnp.float32), conv_in[: length - offset]], axis=0
        )
        earlier_seg = jnp.concatenate(
            [jnp.full((offset,), -1, jnp.int32), segment[: length - offset]]
        )
        same_doc = (earlier_seg == segment).astype(jnp.float32)
        conv_sum = conv_sum + conv_weight[offset][None, :] * earlier * same_doc[:, None]
    activated = jax.nn.silu(conv_sum).reshape(length, head_count, 2 * DK + DV)
    query_rows = activated[:, :, :DK]
    key_rows = activated[:, :, DK : 2 * DK]
    value_rows = activated[:, :, 2 * DK :]
    query_rows = (
        query_rows
        * lax.rsqrt(jnp.sum(query_rows * query_rows, axis=2, keepdims=True) + 1e-06)
        * DK ** (-0.5)
    )
    key_rows = key_rows * lax.rsqrt(jnp.sum(key_rows * key_rows, axis=2, keepdims=True) + 1e-06)
    gate_raw = value_part[:, :, DV : 2 * DV]
    write_rate = jax.nn.sigmoid(value_part[:, :, 2 * DV])
    log_decay = -jnp.exp(decay_log)[None, :] * jax.nn.softplus(
        value_part[:, :, 2 * DV + 1] + step_bias[None, :]
    )
    blocks = length // BLOCK
    query_b = to_blocks(query_rows, blocks)
    key_b = to_blocks(key_rows, blocks)
    value_b = to_blocks(value_rows, blocks)
    rate_b = to_blocks(write_rate, blocks)
    cumulative = jnp.cumsum(to_blocks(log_decay, blocks), axis=2)
    seg_b = segment.reshape(blocks, BLOCK)
    seg_prev = jnp.concatenate([jnp.full((1,), -1, jnp.int32), seg_b[: blocks - 1, BLOCK - 1]])
    places = jnp.arange(BLOCK, dtype=jnp.int32)
    lower_mask = places[:, None] >= places[None, :]
    strict_mask = (places[:, None] > places[None, :]).astype(jnp.float32)
    keep_pair = ((seg_b[:, :, None] == seg_b[:, None, :]) & lower_mask[None])[:, None]
    log_gap = cumulative[:, :, :, None] - cumulative[:, :, None, :]
    decay_pair = jnp.where(keep_pair, jnp.exp(jnp.where(keep_pair, log_gap, 0.0)), 0.0)
    start_keep = (seg_b == seg_prev[:, None])[:, None, :]
    decay_start = jnp.where(start_keep, jnp.exp(cumulative), 0.0)
    end_keep = (seg_b == seg_b[:, BLOCK - 1 :])[:, None, :]
    decay_end = jnp.where(end_keep, jnp.exp(cumulative[:, :, BLOCK - 1 :] - cumulative), 0.0)
    decay_whole = decay_start[:, :, BLOCK - 1]
    key_gram = jnp.einsum("nhik,nhjk->nhij", key_b, key_b, precision=exact_setting)
    system = (
        jnp.eye(BLOCK, dtype=jnp.float32)
        + key_gram * decay_pair * strict_mask * rate_b[:, :, :, None]
    )
    right_side = jnp.concatenate(
        [rate_b[:, :, :, None] * value_b, (rate_b * decay_start)[:, :, :, None] * key_b], axis=3
    )
    solved = jax.scipy.linalg.solve_triangular(system, right_side, lower=True, unit_diagonal=True)
    new_values = solved[:, :, :, :DV]
    weighted = solved[:, :, :, DV:]
    scores = jnp.einsum("nhik,nhjk->nhij", query_b, key_b, precision=exact_setting) * decay_pair

    def advance(carried_state, pieces):
        (
            newest_portion,
            weighted_portion,
            query_fragment,
            key_fragment,
            score_part,
            opening_portion,
            ending_portion,
            entire_portion,
        ) = pieces
        state_update = newest_portion - jnp.einsum(
            "nlq,nqp->nlp", weighted_portion, carried_state, precision=exact_setting
        )
        layer_output = opening_portion[:, :, None] * jnp.einsum(
            "nlq,nqp->nlp", query_fragment, carried_state, precision=exact_setting
        )
        layer_output = layer_output + jnp.einsum(
            "hcj,hjv->hcv", score_part, state_update, precision=exact_setting
        )
        carried_state = entire_portion[:, None, None] * carried_state + jnp.einsum(
            "awo,awm->aom",
            key_fragment * ending_portion[:, :, None],
            state_update,
            precision=exact_setting,
        )
        return (carried_state, layer_output)

    zero_state = jnp.zeros((head_count, DK, DV), jnp.float32)
    final_state, outputs = lax.scan(
        advance,
        zero_state,
        (new_values, weighted, query_b, key_b, scores, decay_start, decay_end, decay_whole),
    )
    outputs = jnp.swapaxes(outputs, 1, 2).reshape(length, head_count, DV)
    normed = outputs * lax.rsqrt(jnp.mean(outputs * outputs, axis=2, keepdims=True) + 1e-05)
    gated_out = normed * gain_head[None, None, :] * jax.nn.silu(gate_raw)
    return gated_out.reshape(length, head_count * DV)


def rows_of(left_mat, right_mat, first_row, row_total):
    return jnp.dot(left_mat, right_mat, preferred_element_type=jnp.float32)


def rows_back(left_mat, right_mat, first_row, row_total):
    return lax.dot_general(
        left_mat, right_mat, (((1,), (1,)), ((), ())), preferred_element_type=jnp.float32
    )


def rows_pair(left_mat, first_w, second_w):
    return jnp.concatenate(
        [
            jnp.dot(left_mat, first_w, preferred_element_type=jnp.float32),
            jnp.dot(left_mat, second_w, preferred_element_type=jnp.float32),
        ],
        axis=1,
    )


def rows_pair_back(first_all, second_all, first_w, second_w, first_row, row_total):
    return rows_back(first_all, first_w, first_row, row_total) + rows_back(
        second_all, second_w, first_row, row_total
    )


def contract_rows(left_mat, right_mat):
    return lax.dot_general(
        left_mat, right_mat, (((0,), (0,)), ((), ())), preferred_element_type=jnp.float32
    )


def token_totals(part_sums):
    return lax.psum(part_sums, "col")


def gather_rows(to_send):
    return lax.all_gather(to_send, "row", axis=0, tiled=True)


def gather_cols(to_send):
    return lax.all_gather(to_send, "col", axis=0, tiled=True)


def reduce_rows(term_fn, row_total):
    return lax.psum_scatter(
        term_fn(jnp.int32(0), lax.axis_size("row") * row_total),
        "row",
        scatter_dimension=0,
        tiled=True,
    )


def reduce_cols(term_fn, row_total):
    return lax.psum_scatter(
        term_fn(jnp.int32(0), lax.axis_size("col") * row_total),
        "col",
        scatter_dimension=0,
        tiled=True,
    )


def norm_forward(values, gain_vec):
    totals = token_totals(jnp.sum(values * values, axis=1))
    inv_scale = lax.rsqrt(totals / D + 1e-05)
    return ((values * inv_scale[:, None] * gain_vec[None, :]).astype(jnp.bfloat16), inv_scale)


def norm_backward(values, gain_vec, inv_scale, normed_grad):
    scaled_grad = normed_grad * gain_vec[None, :]
    inner_sum = token_totals(jnp.sum(scaled_grad * values, axis=1))
    input_part = (
        inv_scale[:, None] * scaled_grad
        - values * (inv_scale * inv_scale * inv_scale * inner_sum / D)[:, None]
    )
    gain_grad = jnp.sum(normed_grad * values * inv_scale[:, None], axis=0)
    return (input_part, gain_grad)


def project_in(normed_rows, first_w, second_w):
    joined = lax.psum_scatter(
        rows_pair(normed_rows, first_w, second_w), "col", scatter_dimension=0, tiled=True
    )
    split_at = first_w.shape[1]
    return (joined[:, :split_at], joined[:, split_at:], (normed_rows, first_w, second_w))


def project_back(first_grad, second_grad, saved_parts, rows_here):
    normed_rows, first_w, second_w = saved_parts
    first_all, second_all = (
        lax.all_gather(first_grad, "col", axis=0, tiled=True),
        lax.all_gather(second_grad, "col", axis=0, tiled=True),
    )
    normed_grad = reduce_rows(
        partial(rows_pair_back, first_all, second_all, first_w, second_w), rows_here
    )
    first_wgrad = contract_rows(normed_rows, first_all)
    second_wgrad = contract_rows(normed_rows, second_all)
    return (normed_grad, first_wgrad, second_wgrad)


def shards(
    inputs,
    gain_attn,
    w_keys,
    w_values,
    conv_weight,
    decay_log,
    step_bias,
    gain_head,
    w_out,
    gain_mlp,
    w_gate,
    w_up,
    w_down,
    seq_lens,
    cotangent,
):
    rows_here = inputs.shape[0]
    row_count = lax.axis_size("row")
    col_count = lax.axis_size("col")
    group_rows = rows_here * row_count
    span_rows = group_rows // col_count
    row_place = lax.axis_index("row")
    col_place = lax.axis_index("col")
    doc_ends = seq_lens[:, 0] + seq_lens[:, 1]
    token_place = row_place * rows_here + jnp.arange(rows_here, dtype=jnp.int32)
    block_match = (token_place // span_rows)[:, None] == jnp.arange(col_count, dtype=jnp.int32)[
        None, :
    ]
    valid_here = jnp.sum(jnp.where(block_match, doc_ends[None, :], 0), axis=1)
    row_mask = (token_place % span_rows < valid_here).astype(jnp.float32)
    own_pick = (jnp.arange(col_count, dtype=jnp.int32) == col_place)[:, None]
    own_lens = jnp.sum(jnp.where(own_pick, seq_lens, 0), axis=0)
    positions = jnp.arange(span_rows, dtype=jnp.int32)
    segment = (positions >= own_lens[0]).astype(jnp.int32) + (
        positions >= own_lens[0] + own_lens[1]
    ).astype(jnp.int32)
    resid_in = inputs.astype(jnp.float32)
    normed_attn, scale_attn = norm_forward(resid_in, gain_attn)
    normed_attn_rows = gather_rows(normed_attn)
    keys_proj, values_proj, saved_attn = project_in(normed_attn_rows, w_keys, w_values)

    def mixer_local(keys_in, values_in, conv_in, decay_in, bias_in, head_in):
        return delta_mixer(keys_in, values_in, conv_in, decay_in, bias_in, head_in, segment)

    mixed_out, mixer_pull = jax.vjp(
        mixer_local, keys_proj, values_proj, conv_weight, decay_log, step_bias, gain_head
    )
    mixed_rows = gather_cols(mixed_out.astype(jnp.bfloat16))
    attn_out = reduce_rows(partial(rows_of, mixed_rows, w_out), rows_here)
    resid_mid = resid_in + attn_out
    normed_mlp, scale_mlp = norm_forward(resid_mid, gain_mlp)
    normed_mlp_rows = gather_rows(normed_mlp)
    gate_pre, up_pre, saved_mlp = project_in(normed_mlp_rows, w_gate, w_up)
    gate_act = jax.nn.silu(gate_pre)
    hidden = (gate_act * up_pre).astype(jnp.bfloat16)
    hidden_rows = gather_cols(hidden)
    mlp_out = reduce_rows(partial(rows_of, hidden_rows, w_down), rows_here)
    result = resid_mid + mlp_out
    out_grad = cotangent * row_mask[:, None]
    mlp_grad_rows = gather_rows(out_grad.astype(jnp.bfloat16))
    grad_w_down = contract_rows(hidden_rows, mlp_grad_rows)
    hidden_grad = reduce_cols(partial(rows_back, mlp_grad_rows, w_down), span_rows)
    sigmoid_gate = jax.nn.sigmoid(gate_pre)
    gate_grad = (
        hidden_grad * up_pre * sigmoid_gate * (1.0 + gate_pre * (1.0 - sigmoid_gate))
    ).astype(jnp.bfloat16)
    up_grad = (hidden_grad * gate_act).astype(jnp.bfloat16)
    normed_mlp_grad, grad_w_gate, grad_w_up = project_back(gate_grad, up_grad, saved_mlp, rows_here)
    mid_grad, grad_gain_mlp = norm_backward(resid_mid, gain_mlp, scale_mlp, normed_mlp_grad)
    resid_grad = out_grad + mid_grad
    attn_grad_rows = gather_rows(resid_grad.astype(jnp.bfloat16))
    grad_w_out = contract_rows(mixed_rows, attn_grad_rows)
    mixed_grad = reduce_cols(partial(rows_back, attn_grad_rows, w_out), span_rows)
    keys_grad, values_grad, grad_conv, grad_decay_log, grad_step_bias, grad_gain_head = mixer_pull(
        mixed_grad
    )
    normed_attn_grad, grad_w_keys, grad_w_values = project_back(
        keys_grad.astype(jnp.bfloat16), values_grad.astype(jnp.bfloat16), saved_attn, rows_here
    )
    input_part, grad_gain_attn = norm_backward(resid_in, gain_attn, scale_attn, normed_attn_grad)
    input_grad = resid_grad + input_part
    grad_conv, grad_decay_log, grad_step_bias, grad_gain_head = (
        lax.psum(grad_conv.astype(jnp.bfloat16), "col").astype(jnp.float32),
        lax.psum(grad_decay_log.astype(jnp.bfloat16), "col").astype(jnp.float32),
        lax.psum(grad_step_bias.astype(jnp.bfloat16), "col").astype(jnp.float32),
        lax.psum(grad_gain_head.astype(jnp.bfloat16), "col").astype(jnp.float32),
    )
    grad_gain_attn, grad_gain_mlp, grad_gain_head = lax.psum(
        (grad_gain_attn, grad_gain_mlp, grad_gain_head), ("dp", "row")
    )
    (
        grad_w_keys,
        grad_w_values,
        grad_conv,
        grad_decay_log,
        grad_step_bias,
        grad_w_out,
        grad_w_gate,
        grad_w_up,
        grad_w_down,
    ) = lax.psum(
        (
            grad_w_keys,
            grad_w_values,
            grad_conv,
            grad_decay_log,
            grad_step_bias,
            grad_w_out,
            grad_w_gate,
            grad_w_up,
            grad_w_down,
        ),
        "dp",
    )
    return (
        result,
        input_grad,
        grad_gain_attn,
        grad_w_keys,
        grad_w_values,
        grad_conv,
        grad_decay_log,
        grad_step_bias,
        grad_gain_head,
        grad_w_out,
        grad_gain_mlp,
        grad_w_gate,
        grad_w_up,
        grad_w_down,
    )


def solution(mesh):
    in_specs = (
        P(("dp", "row"), "col"),
        P("col"),
        P("col", "row"),
        P("col", "row"),
        P(None, "row"),
        P("row"),
        P("row"),
        P(),
        P("row", "col"),
        P("col"),
        P("col", "row"),
        P("col", "row"),
        P("row", "col"),
        P("dp", None),
        P(("dp", "row"), "col"),
    )
    out_specs = (
        P(("dp", "row"), "col"),
        P(("dp", "row"), "col"),
        P("col"),
        P("col", "row"),
        P("col", "row"),
        P(None, "row"),
        P("row"),
        P("row"),
        P(),
        P("row", "col"),
        P("col"),
        P("col", "row"),
        P("col", "row"),
        P("row", "col"),
    )
    return jax.shard_map(shards, mesh=mesh, in_specs=in_specs, out_specs=out_specs, check_vma=False)
```

profile of v0, /device:TPU:0, one launch (start us, length us, event | category | flops | bytes accessed | tf_op | source)
XLA Modules:
  0.0 3402.7 jit_solution(10134594914217518670)
XLA Ops:
  8.4 5.8 psum.140
  16.4 10.9 all-gather.11.cloned.1.call-done
  27.4 11.9 fusion.186
  43.7 11.2 pad_maximum_fusion
  62.3 138.7 %reduce-scatter.9.cloned.1.call-done = f32[256,6160]{0,1:T(8,128)} async-done(((f32[512,6160]{0,1:T(8,128)}), f32[256,6160]{0,1:T(8,128)}) %reduce-scatter.9.cloned.1.call-update) | async-done | bytes 6307856 | tf_op jit(solution)/shard_map/reduce_scatter | solution.py:208
  220.9 7.6 fusion.83
  252.2 158.4 %custom-call.10 = f32[4,8,1,64,64]{3,4,2,1,0:T(8,128)S(1)} custom-call(f32[4,8,1,64,64]{4,3,2,1,0:T(8,128)} %get-tuple-element.1110), custom_call_target="InvertDiagBlocksLowerTriangular" | custom-call | tf_op jit(solution)/shard_map/jvp(jit(_solve_triangular))/vmap(vmap())/triangular_solve | solution.py:83
  423.7 49.0 %while.58 = (s32[]{:T(128)}, f32[8,128,256]{2,1,0:T(8,128)S(1)}, f32[4,8,64,256]{3,1,2,0:T(8,128)}, f32[4,8,128,256]{3,2,1,0:T(8,128)}, f32[4,8,64,256]{3,2,1,0:...) while((s32[]{:T(128)}, f32[8,128,256]{2,1,0:T(8,128)S(1)}, ...), condition=%wide.region_8.9_spmd.clone, body=%wide.region_7.8_spmd.clone.sunk | while | flops 706740224 | bytes 17863016 | solution.py:117
  482.5 33.0 all-gather.13.cloned.1.call-done
  515.5 6.5 fusion.187
  523.4 8.4 reduce-scatter.11.cloned.1.call-done
  544.1 8.5 fusion.191
  556.4 8.6 fusion.189
  565.0 8.4 fusion.188
  573.4 10.0 pad_maximum_fusion.1
  583.7 46.8 %reduce-scatter.17.cloned.1.call-done = f32[256,2752]{0,1:T(8,128)} async-done(((f32[512,2752]{0,1:T(8,128)}), f32[256,2752]{0,1:T(8,128)}) %reduce-scatter.17.cloned.1.call-update) | async-done | bytes 2818064 | tf_op jit(solution)/shard_map/reduce_scatter | solution.py:182
  630.5 133.3 %reduce-scatter.13.cloned.1.call-done = f32[256,5504]{0,1:T(8,128)} async-done(((f32[512,5504]{0,1:T(8,128)}), f32[256,5504]{0,1:T(8,128)}) %reduce-scatter.13.cloned.1.call-update) | async-done | bytes 5636112 | tf_op jit(solution)/shard_map/reduce_scatter | solution.py:208
  770.8 40.0 %all-gather.21.cloned.1.call-done = bf16[512,2752]{0,1:T(8,128)(2,1)} async-done(((bf16[256,2752]{0,1:T(8,128)(2,1)}), bf16[512,2752]{0,1:T(8,128)(2,1)}) %all-gather.21.cloned.1.call-update) | async-done | bytes 2818064 | tf_op jit(solution)/shard_map/all_gather | solution.py:218
  810.8 7.9 fusion.192
  818.8 35.3 %all-gather.23.cloned.1.call-done = bf16[512,2752]{0,1:T(8,128)(2,1)} async-done(((bf16[256,2752]{0,1:T(8,128)(2,1)}), bf16[512,2752]{0,1:T(8,128)(2,1)}) %all-gather.23.cloned.1.call-update) | async-done | bytes 2818064 | tf_op jit(solution)/shard_map/all_gather | solution.py:219
  854.0 8.5 convolution_add_fusion.6
  862.6 34.7 %all-gather.17.cloned.1.call-done = bf16[512,2752]{0,1:T(8,128)(2,1)} async-done(((bf16[256,2752]{0,1:T(8,128)(2,1)}), bf16[512,2752]{0,1:T(8,128)(2,1)}) %all-gather.17.cloned.1.call-update) | async-done | bytes 2818064 | tf_op jit(solution)/shard_map/all_gather | solution.py:169
  897.4 7.9 fusion.190
  916.7 6.7 reduce-scatter.15.cloned.1.call-done
  926.9 10.3 all-gather.25.cloned.1.call-done
  937.2 6.9 fusion.193
  944.6 55.2 %reduce-scatter.21.cloned.1.call-done = f32[256,2048]{1,0:T(8,128)} async-done(((f32[512,2048]{1,0:T(8,128)}), f32[256,2048]{1,0:T(8,128)}) %reduce-scatter.21.cloned.1.call-update) | async-done | bytes 2097168 | tf_op jit(solution)/shard_map/reduce_scatter | solution.py:182
  1002.6 9.2 multiply_reduce_fusion.3
  1022.7 93.7 %while.59 = (s32[]{:T(128)}, f32[8,128,256]{2,1,0:T(8,128)S(1)}, f32[4,8,64,256]{3,2,1,0:T(8,128)}, f32[4,8,64,128]{3,2,1,0:T(8,128)}, f32[4,8,64,128]{3,2,1,0:T...) while((s32[]{:T(128)}, f32[8,128,256]{2,1,0:T(8,128)S(1)}, ...), condition=%wide.region_26.27_spmd.clone, body=%wide.region_22.26_spmd.clone.sunk | while | flops 1412758528 | bytes 38578692 | solution.py:117
  1162.1 6.3 multiply_reduce_fusion.2
  1193.3 54.2 %all-gather.29.cloned.1.call-done = bf16[512,4112]{0,1:T(8,128)(2,1)} async-done(((bf16[256,4112]{0,1:T(8,128)(2,1)}), bf16[512,4112]{0,1:T(8,128)(2,1)}) %all-gather.29.cloned.1.call-update) | async-done | bytes 4210704 | tf_op jit(solution)/shard_map/all_gather | solution.py:219
  1247.6 10.8 fusion.194
  1258.3 24.4 all-gather.27.cloned.1.call-done
  1282.7 7.2 convolution_add_fusion.5
  1290.2 8.0 fusion.199
  1298.2 6.0 fusion.200
  1304.2 6.0 fusion.197
  1316.0 5.8 fusion.195
  1321.8 8.5 fusion.198
  1331.4 7.2 all-reduce.26
  1338.7 43.1 %all-reduce.31 = (f32[4,4096]{1,0:T(4,128)}, f32[8]{0:T(128)}, f32[8]{0:T(128)}) all-reduce(bf16[4,4096]{1,0:T(4,128)(2,1)S(1)} %get-tuple-element.1053, bf16[8]{0:T(256)(128)(2,1)S(1)} %get-tuple-element.1054, bf16[8]{0:T(256)(128)(2,1)S(1)} %get-tuple-element.1055), channel_id=1, replica_groups=mesh['dp'=8,'row'=2,'col'=2] {'dp'}, use_global_device_ids=true, to_apply=%region_48.49 | all-reduce | flops 16400 | bytes 98400 | tf_op jit(solution)/shard_map/psum | solution.py:330
  1388.3 34.0 all-reduce.23
  1424.8 1914.7 %all-reduce.30.cloned.1.call-done = (f32[1024,2048]{1,0:T(8,128)}, f32[1024,4112]{0,1:T(8,128)}, f32[2048,1024]{1,0:T(8,128)}, f32[1024,2752]{0,1:T(8,128)}, f32[1024,2752]{0,1:T(8,128)}, /*index=5*/f32[2752,1024]{1,0:T(8,128)}) async-done(((f32[1024,2048]{1,0:T(8,128)}, f32[1024,4112]{0,1:T(8,128)}, f32[2048,1024]{1,0:T(8,128)}, f32[1024,2752]{0,1:T(8,128)}, f32[1024,2752]{0,1:T(8,128)}, ...) | async-done | bytes 67436560 | tf_op jit(solution)/shard_map/psum | solution.py:330
  3339.5 8.0 copy.568
  3347.5 11.9 copy.569
  3362.8 11.0 copy.571
  3373.8 11.0 copy.572
  3384.8 11.0 copy.573
  (576 shorter events, 365.0 us)
Async XLA Ops:
  7.2 20.2 all-gather.11.cloned.1.call-start
  14.3 24.9 copy-start.90
  14.3 24.9 copy-start.80
  16.4 184.7 %reduce-scatter.9.cloned.1.call-start = ((), (), s32[]{:S(2)}) async-start(), calls=%async_computation.9 | async-start | bytes 18923520 | tf_op jit(solution)/shard_map/reduce_scatter | solution.py:208
  27.4 11.9 copy-start.104
  27.4 11.9 copy-start.108
  54.9 460.6 %all-gather.13.cloned.1.call-start = ((), (), s32[]{:S(2)}) async-start(), calls=%async_computation.10 | async-start | bytes 3145728 | tf_op jit(solution)/shard_map/all_gather | solution.py:169
  59.8 157.5 %copy-start.82 = (f32[256]{0:T(256)}, f32[256]{0:T(256)S(1)}, u32[]{:S(2)}) copy-start(f32[256]{0:T(256)S(1)} %compare_convert_fusion.3) | copy-start | bytes 3076
  60.6 156.8 %copy-start.84 = (f32[256]{0:T(256)}, f32[256]{0:T(256)S(1)}, u32[]{:S(2)}) copy-start(f32[256]{0:T(256)S(1)} %get-tuple-element.1120) | copy-start | bytes 3076
  60.6 156.8 %copy-start.86 = (f32[256]{0:T(256)}, f32[256]{0:T(256)S(1)}, u32[]{:S(2)}) copy-start(f32[256]{0:T(256)S(1)} %get-tuple-element.1119) | copy-start | bytes 3076
  60.8 175.8 %copy-start.99 = (f32[8]{0:T(128)}, f32[8]{0:T(128)S(1)}, u32[]{:S(2)}) copy-start(f32[8]{0:T(128)S(1)} %exponential_negate_fusion) | copy-start | bytes 100
  62.0 176.3 %copy-start.93 = (pred[4,64]{1,0:T(4,128)(4,1)}, pred[4,64]{1,0:T(4,128)(4,1)S(1)}, u32[]{:S(2)}) copy-start(pred[4,64]{1,0:T(4,128)(4,1)S(1)} %get-tuple-element.1121) | copy-start | bytes 772
  62.3 155.1 %copy-start.56 = (f32[1,4096]{1,0:T(1,128)}, f32[1,4096]{1,0:T(1,128)S(1)}, u32[]{:S(2)}) copy-start(f32[1,4096]{1,0:T(1,128)S(1)} %get-tuple-element.1105) | copy-start | bytes 49156
  62.3 155.1 %copy-start.58 = (f32[1,4096]{1,0:T(1,128)}, f32[1,4096]{1,0:T(1,128)S(1)}, u32[]{:S(2)}) copy-start(f32[1,4096]{1,0:T(1,128)S(1)} %get-tuple-element.1107) | copy-start | bytes 49156
  62.3 155.1 %copy-start.60 = (f32[1,4096]{1,0:T(1,128)}, f32[1,4096]{1,0:T(1,128)S(1)}, u32[]{:S(2)}) copy-start(f32[1,4096]{1,0:T(1,128)S(1)} %get-tuple-element.1108) | copy-start | bytes 49156
  62.3 155.1 %copy-start.62 = (f32[1,4096]{1,0:T(1,128)}, f32[1,4096]{1,0:T(1,128)S(1)}, u32[]{:S(2)}) copy-start(f32[1,4096]{1,0:T(1,128)S(1)} %get-tuple-element.1106) | copy-start | bytes 49156
  210.5 25.9 copy-start.70
  210.5 26.0 copy-start.68
  482.3 39.8 %copy-start.89 = (s32[2,3]{1,0:T(2,128)S(1)}, s32[2,3]{1,0:T(2,128)}, u32[]{:S(2)}) copy-start(s32[2,3]{1,0:T(2,128)} %param.32) | copy-start | bytes 76
  482.3 49.5 %reduce-scatter.11.cloned.1.call-start = ((), (), s32[]{:S(2)}) async-start(), calls=%async_computation.11 | async-start | bytes 3145728 | tf_op jit(solution)/shard_map/reduce_scatter | solution.py:173
  482.5 39.9 %copy-start.44 = (f32[256,1024]{1,0:T(8,128)S(1)}, f32[256,1024]{1,0:T(8,128)}, u32[]{:S(2)}) copy-start(f32[256,1024]{1,0:T(8,128)} %param.33) | copy-start | bytes 3145732
  522.0 16.2 copy-start.75
  522.0 22.1 all-gather.19.cloned.1.call-start
  523.3 33.0 all-gather.15.cloned.1.call-start
  539.2 91.3 %reduce-scatter.17.cloned.1.call-start = ((), (), s32[]{:S(2)}) async-start(), calls=%async_computation.17 | async-start | bytes 8454144 | tf_op jit(solution)/shard_map/reduce_scatter | solution.py:182
  552.7 211.1 %reduce-scatter.13.cloned.1.call-start = ((), (), s32[]{:S(2)}) async-start(), calls=%async_computation.13 | async-start | bytes 16908288 | tf_op jit(solution)/shard_map/reduce_scatter | solution.py:208
  583.4 227.4 %all-gather.21.cloned.1.call-start = ((), (), s32[]{:S(2)}) async-start(), calls=%async_computation.18 | async-start | bytes 4227072 | tf_op jit(solution)/shard_map/all_gather | solution.py:218
  769.5 84.6 %all-gather.23.cloned.1.call-start = ((), (), s32[]{:S(2)}) async-start(), calls=%async_computation.19 | async-start | bytes 4227072 | tf_op jit(solution)/shard_map/all_gather | solution.py:219
  770.0 127.3 %all-gather.17.cloned.1.call-start = ((), (), s32[]{:S(2)}) async-start(), calls=%async_computation.14 | async-start | bytes 4227072 | tf_op jit(solution)/shard_map/all_gather | solution.py:169
  770.8 138.9 %reduce-scatter.19.cloned.1.call-start = ((), (), s32[]{:S(2)}) async-start(), calls=%async_computation.20 | async-start | bytes 3145728 | tf_op jit(solution)/shard_map/reduce_scatter | solution.py:173
  862.6 60.8 %reduce-scatter.15.cloned.1.call-start = ((), (), s32[]{:S(2)}) async-start(), calls=%async_computation.15 | async-start | bytes 3145728 | tf_op jit(solution)/shard_map/reduce_scatter | solution.py:173
  905.3 18.1 copy-start.45
  905.4 31.9 all-gather.25.cloned.1.call-start
  926.8 72.9 %reduce-scatter.21.cloned.1.call-start = ((), (), s32[]{:S(2)}) async-start(), calls=%async_computation.22 | async-start | bytes 6291456 | tf_op jit(solution)/shard_map/reduce_scatter | solution.py:182
  944.1 58.5 %copy-start.92 = (f32[256]{0:T(256)S(1)}, f32[256]{0:T(256)}, u32[]{:S(2)}) copy-start(f32[256]{0:T(256)} %param.26) | copy-start | bytes 3076
  944.1 303.4 %all-gather.29.cloned.1.call-start = ((), (), s32[]{:S(2)}) async-start(), calls=%async_computation.24 | async-start | bytes 6316032 | tf_op jit(solution)/shard_map/all_gather | solution.py:219
  1190.5 92.2 %all-gather.27.cloned.1.call-start = ((), (), s32[]{:S(2)}) async-start(), calls=%async_computation.23 | async-start | bytes 3145728 | tf_op jit(solution)/shard_map/all_gather | solution.py:218
  1193.3 188.5 %reduce-scatter.23.cloned.1.call-start = ((), (), s32[]{:S(2)}) async-start(), calls=%async_computation.25 | async-start | bytes 3145728 | tf_op jit(solution)/shard_map/reduce_scatter | solution.py:173
  1258.3 31.9 copy-start.112
  1290.0 2049.5 %all-reduce.30.cloned.1.call-start = ((), (), s32[]{:S(2)}) async-start(), calls=%async_computation.26 | async-start | bytes 134873088 | tf_op jit(solution)/shard_map/psum | solution.py:330
  1330.4 51.5 %copy-start.29 = (bf16[256,1024]{1,0:T(8,128)(2,1)S(1)}, bf16[256,1024]{1,0:T(8,128)(2,1)}, u32[]{:S(2)}) copy-start(bf16[256,1024]{1,0:T(8,128)(2,1)} %param.19) | copy-start | bytes 1572868
  1330.4 51.5 %copy-start.76 = (f32[1024]{0:T(1024)S(1)}, f32[1024]{0:T(1024)}, u32[]{:S(2)}) copy-start(f32[1024]{0:T(1024)} %param.20) | copy-start | bytes 12292
  1330.4 51.4 %copy-start.81 = (f32[256]{0:T(256)S(1)}, f32[256]{0:T(256)}, u32[]{:S(2)}) copy-start(f32[256]{0:T(256)} %copy-done.80) | copy-start | bytes 3076
  1330.4 57.9 %copy-start.79 = (f32[1024]{0:T(1024)S(1)}, f32[1024]{0:T(1024)}, u32[]{:S(2)}) copy-start(f32[1024]{0:T(1024)} %get-tuple-element.952) | copy-start | bytes 12292
  1330.4 91.9 %copy-start.91 = (f32[256]{0:T(256)S(1)}, f32[256]{0:T(256)}, u32[]{:S(2)}) copy-start(f32[256]{0:T(256)} %copy-done.90) | copy-start | bytes 3076
  1330.4 91.9 %copy-start.48 = (f32[256,1024]{1,0:T(8,128)S(1)}, f32[256,1024]{1,0:T(8,128)}, u32[]{:S(2)}) copy-start(f32[256,1024]{1,0:T(8,128)} %get-tuple-element.1065) | copy-start | bytes 3145732
  3339.5 20.0 slice-start.1
  3347.5 11.9 slice-start.2
  (98 other events, 457.8 us)
Sparse Core Ops, SparseCore 0:
  16.5 10.8 all-gather.10
  55.0 145.9 reduce-scatter.8
  482.4 33.0 all-gather.12
  522.1 9.6 reduce-scatter.10
  533.8 10.1 all-gather.18
  546.1 10.1 all-gather.14
  559.4 71.0 reduce-scatter.16
  633.4 130.3 reduce-scatter.12
  769.6 41.2 all-gather.20
  812.8 41.1 all-gather.22
  856.1 41.1 all-gather.16
  900.1 9.6 reduce-scatter.18
  912.6 10.7 reduce-scatter.14
  927.0 10.2 all-gather.24
  944.3 55.4 reduce-scatter.20
  1190.6 56.8 all-gather.28
  1249.6 33.0 all-gather.26
  1290.1 9.5 reduce-scatter.22
  1330.6 2008.8 all-reduce.29
where the time goes:
time: 3410 us; the launch traced here: 3400 us
  waiting for transfers between devices  2560 us (75%)
  other arithmetic  294 us (9%)
  matrix products  272 us (8%)
  local copies, waits for them, and re-layouts  151 us (4%)
  blocking collectives  105 us (3%)
    psum x1, waiting for transfers between devices, shards(): lax.psum((grad_w_keys, grad_w_values, grad_conv, grad_decay_log, grad_ste...  1910 us
    reduce_scatter x2, waiting for transfers between devices, project_in(): lax.psum_scatter(rows_pair(normed_rows, first_w, second_w), 'col', scatte...  272 us
    another operation x3, other arithmetic, delta_mixer(): jax.scipy.linalg.solve_triangular(system, right_side, lower=True, unit_di...  158 us
    reduce_scatter x2, waiting for transfers between devices, reduce_cols(): lax.psum_scatter(term_fn(jnp.int32(0), lax.axis_size('col') * row_total),...  102 us
    all_gather x2, waiting for transfers between devices, project_back(): lax.all_gather(second_grad, 'col', axis=0, tiled=True)  89.5 us
    unnamed x248, local copies, waits for them, and re-layouts  74.5 us
  transfers between devices with their start and end apart: 19, of which 18 were waited for; matrix products, arithmetic and copies ran while one was open for 4% of the time, Pallas kernels for 0%

commit v1 on v0

v1 whole, which is shorter than its diff:
```python
from functools import partial

import jax
import jax.numpy as jnp
from jax import lax
from jax.experimental import pallas as pl
from jax.experimental.pallas import tpu as pltpu
from jax.sharding import PartitionSpec as P

DK = 128
DV = 256
KCONV = 4
HEAD_IN = 2 * DK + DV
HEAD_VALUES = 2 * DV + 2
F32 = jnp.float32
BF16 = jnp.bfloat16

NN = (((1,), (0,)), ((), ()))
NT = (((1,), (1,)), ((), ()))
TN = (((0,), (0,)), ((), ()))


def halves(a):
    high = a.astype(BF16)
    return high, (a - high.astype(F32)).astype(BF16)


def dot3(a, b, dims=NN):
    a_high, a_low = a if isinstance(a, tuple) else halves(a)
    b_high, b_low = b if isinstance(b, tuple) else halves(b)
    left = dims[0][0][0]
    right = dims[0][1][0]
    return lax.dot_general(
        jnp.concatenate([a_high, a_high, a_low], axis=left),
        jnp.concatenate([b_high, b_low, b_high], axis=right),
        dims,
        preferred_element_type=F32,
    )


def sigmoid(v):
    return 1.0 / (1.0 + jnp.exp(-v))


def softplus(v):
    return jnp.maximum(v, 0.0) + jnp.log(1.0 + jnp.exp(-jnp.abs(v)))


def grid_ids(n):
    return (
        lax.broadcasted_iota(jnp.int32, (n, n), 0),
        lax.broadcasted_iota(jnp.int32, (n, n), 1),
    )


def head_pieces(head, pre, window, meta, conv_w, decay_log, step_bias):
    rows = pre.shape[0]
    picked = pltpu.roll(window, window.shape[1] - 2 * head, 1)
    conv_in = jnp.concatenate([pre, picked[:, :DV]], axis=1)
    gate = picked[:, DV : 2 * DV]
    rate = sigmoid(picked[:, 2 * DV : 2 * DV + 1])
    step_in = picked[:, 2 * DV + 1 : 2 * DV + 2] + step_bias
    strength = jnp.exp(jnp.full((1, 1), decay_log, F32))
    log_decay = -strength * softplus(step_in)
    conv = conv_w[0:1, :] * conv_in
    for s in range(1, KCONV):
        conv = conv + conv_w[s : s + 1, :] * (
            pltpu.roll(conv_in, s, 0) * meta[:, s : s + 1]
        )
    sig = sigmoid(conv)
    act = conv * sig
    q_act, k_act, values = act[:, :DK], act[:, DK : 2 * DK], act[:, 2 * DK :]
    q_scale = lax.rsqrt(jnp.sum(q_act * q_act, axis=1, keepdims=True) + 1e-06)
    k_scale = lax.rsqrt(jnp.sum(k_act * k_act, axis=1, keepdims=True) + 1e-06)
    query = q_act * (q_scale * DK ** (-0.5))
    key = k_act * k_scale
    row_id, col_id = grid_ids(rows)
    after = row_id > col_id
    d_high = log_decay.astype(BF16).astype(F32)
    d_mid = (log_decay - d_high).astype(BF16).astype(F32)
    d_low = log_decay - d_high - d_mid
    lower = jnp.where(row_id >= col_id, 1.0, 0.0).astype(BF16)
    terms = jnp.concatenate(
        [jnp.where(after, d, 0.0).astype(BF16) for d in (d_high, d_mid, d_low)], axis=0
    )
    gap = lax.dot_general(
        jnp.concatenate([lower, lower, lower], axis=1), terms, NN, preferred_element_type=F32
    )
    return dict(
        conv_in=conv_in, gate=gate, rate=rate, step_in=step_in, strength=strength,
        log_decay=log_decay, conv=conv, sig=sig, q_act=q_act, k_act=k_act, values=values,
        q_scale=q_scale, k_scale=k_scale, query=query, key=key, gap=gap, after=after,
        row_id=row_id, col_id=col_id,
    )


def unit_lower_inverse(strict, row_id, col_id):
    n = strict.shape[0]
    differ = row_id ^ col_id
    below = row_id > col_id
    inverse = jnp.where(row_id == col_id, 1.0, 0.0) - jnp.where(
        (differ == 1) & below, strict, 0.0
    )
    size = 2
    while size < n:
        part = jnp.where((differ >= size) & (differ < 2 * size) & below, strict, 0.0)
        split = halves(inverse)
        inverse = inverse - dot3(split, dot3(part, split))
        size *= 2
    return inverse


def pair_mask(seg_col, seg_row, row_id, col_id):
    return jnp.where((seg_col == seg_row) & (row_id >= col_id), 1.0, 0.0)


def fill_values(own_ref, other_ref, values_ref):
    width = own_ref.shape[1]
    values_ref[:, pl.ds(values_ref.shape[1] - 128, 128)] = jnp.zeros(
        (values_ref.shape[0], 128), F32
    )
    values_ref[:, :width] = own_ref[...] + other_ref[...].astype(F32)


def mixer_forward_kernel(
    decay_ref, bias_ref, pk_ref, rk_ref, pv_ref, rv_ref, meta_ref, seg_ref, conv_ref, gain_ref,
    mixed_ref, inverse_ref,
    values_ref, mask_ref,
):
    head = pl.program_id(0)
    rows = pk_ref.shape[0]

    @pl.when(head == 0)
    def _():
        fill_values(pv_ref, rv_ref, values_ref)
        row_id, col_id = grid_ids(rows)
        mask_ref[...] = pair_mask(meta_ref[:, 0:1], seg_ref[0:1, :], row_id, col_id)

    window = values_ref[:, pl.ds(pl.multiple_of(head * (2 * DV), 128), 2 * DV + 128)]
    p = head_pieces(
        head, pk_ref[...] + rk_ref[...].astype(F32), window, meta_ref[...], conv_ref[...],
        decay_ref[head], bias_ref[head],
    )
    decay_pair = jnp.exp(p["gap"]) * mask_ref[...]
    key = halves(p["key"])
    gram = dot3(key, key, NT)
    strict = jnp.where(p["after"], gram * decay_pair, 0.0) * p["rate"]
    inverse = unit_lower_inverse(strict, p["row_id"], p["col_id"])
    inverse_ref[0] = inverse
    updates = dot3(inverse, p["rate"] * p["values"])
    scores = dot3(p["query"], key, NT) * decay_pair
    out = dot3(scores, updates)
    out = out * lax.rsqrt(jnp.mean(out * out, axis=1, keepdims=True) + 1e-05)
    gate = p["gate"]
    mixed_ref[...] = (out * gain_ref[...] * (gate * sigmoid(gate))).astype(BF16)


def mixer_backward_kernel(
    decay_ref, bias_ref, pk_ref, rk_ref, pv_ref, rv_ref, meta_ref, seg_ref, conv_ref, gain_ref,
    inverse_ref, pg_ref, rg_ref,
    dk_ref, dv_ref, small_ref,
    values_ref, mask_ref, grads_ref,
):
    head = pl.program_id(0)
    rows = pk_ref.shape[0]

    @pl.when(head == 0)
    def _():
        fill_values(pv_ref, rv_ref, values_ref)
        row_id, col_id = grid_ids(rows)
        mask_ref[...] = pair_mask(meta_ref[:, 0:1], seg_ref[0:1, :], row_id, col_id)
        grads_ref[...] = jnp.zeros_like(grads_ref)

    lanes = pl.ds(pl.multiple_of(head * (2 * DV), 128), 2 * DV + 128)
    meta = meta_ref[...]
    conv_w = conv_ref[...]
    p = head_pieces(
        head, pk_ref[...] + rk_ref[...].astype(F32), values_ref[:, lanes], meta, conv_w,
        decay_ref[head], bias_ref[head],
    )
    rate, values, gate = p["rate"], p["values"], p["gate"]
    gain = gain_ref[...]
    decay_pair = jnp.exp(p["gap"]) * mask_ref[...]
    decay_strict = jnp.where(p["after"], decay_pair, 0.0)
    key, query = halves(p["key"]), halves(p["query"])
    gram = dot3(key, key, NT) * decay_strict
    inverse = halves(inverse_ref[0])
    updates = halves(dot3(inverse, rate * values))
    scores = dot3(query, key, NT) * decay_pair
    scores_split = halves(scores)
    out = dot3(scores_split, updates)
    grad = pg_ref[...] + rg_ref[...].astype(F32)
    scale = lax.rsqrt(jnp.mean(out * out, axis=1, keepdims=True) + 1e-05)
    normed = out * scale
    gate_sig = sigmoid(gate)
    gate_act = gate * gate_sig
    d_gain = jnp.sum(grad * normed * gate_act, axis=0, keepdims=True)
    d_gate = grad * normed * gain * (gate_sig * (1.0 + gate * (1.0 - gate_sig)))
    d_normed = grad * gain * gate_act
    d_out = scale * d_normed - normed * (
        scale * jnp.mean(d_normed * normed, axis=1, keepdims=True)
    )
    d_out = halves(d_out)
    d_scores = dot3(d_out, updates, NT)
    d_updates = dot3(scores_split, d_out, TN)
    d_right = dot3(inverse, d_updates, TN)
    d_strict = -dot3(d_right, updates, NT)
    d_gap = d_scores * scores + d_strict * gram * rate
    d_qk = halves(d_scores * decay_pair)
    d_gram = halves(d_strict * decay_strict * rate)
    d_query = dot3(d_qk, key)
    d_key = dot3(d_qk, query, TN) + dot3(d_gram, key) + dot3(d_gram, key, TN)
    d_rate = jnp.sum(d_strict * gram, axis=1, keepdims=True) + jnp.sum(
        d_right * values, axis=1, keepdims=True
    )
    d_values = rate * d_right
    gap_high, gap_low = halves(d_gap)
    upper = jnp.where(p["col_id"] >= p["row_id"], 1.0, 0.0).astype(BF16)
    spans = lax.dot_general(
        jnp.concatenate([upper, upper], axis=1),
        jnp.concatenate([gap_high, gap_low], axis=0),
        NN,
        preferred_element_type=F32,
    )
    d_log = jnp.sum(jnp.where(p["after"], spans, 0.0), axis=1, keepdims=True)
    d_step = -p["strength"] * d_log * sigmoid(p["step_in"])
    d_decay = jnp.sum(d_log * p["log_decay"], axis=0, keepdims=True)
    d_bias = jnp.sum(d_step, axis=0, keepdims=True)
    d_rate = d_rate * rate * (1.0 - rate)
    q_scale, k_scale = p["q_scale"], p["k_scale"]
    d_query = d_query * DK ** (-0.5)
    d_q_act = q_scale * d_query - p["q_act"] * (
        q_scale * q_scale * q_scale * jnp.sum(d_query * p["q_act"], axis=1, keepdims=True)
    )
    d_k_act = k_scale * d_key - p["k_act"] * (
        k_scale * k_scale * k_scale * jnp.sum(d_key * p["k_act"], axis=1, keepdims=True)
    )
    sig, conv, conv_in = p["sig"], p["conv"], p["conv_in"]
    d_conv = jnp.concatenate([d_q_act, d_k_act, d_values], axis=1) * (
        sig * (1.0 + conv * (1.0 - sig))
    )
    d_in = conv_w[0:1, :] * d_conv
    tap_grads = [jnp.sum(d_conv * conv_in, axis=0, keepdims=True)]
    for s in range(1, KCONV):
        masked = d_conv * meta[:, s : s + 1]
        tap_grads.append(
            jnp.sum(masked * pltpu.roll(conv_in, s, 0), axis=0, keepdims=True)
        )
        d_in = d_in + conv_w[s : s + 1, :] * pltpu.roll(masked, rows - s, 0)
    dk_ref[...] = d_in[:, : 2 * DK].astype(BF16)
    lane = lax.broadcasted_iota(jnp.int32, (rows, 128), 1)
    last = jnp.where(lane == 0, d_rate, jnp.where(lane == 1, d_step, 0.0))
    wide = jnp.concatenate([d_in[:, 2 * DK :], d_gate, last], axis=1)
    grads_ref[:, lanes] = grads_ref[:, lanes] + pltpu.roll(wide, 2 * head, 1)
    lane_row = lax.broadcasted_iota(jnp.int32, (1, HEAD_IN - DV), 1)
    ends = jnp.where(lane_row == 0, d_decay, jnp.where(lane_row == 1, d_bias, 0.0))
    small_ref[0] = jnp.concatenate(
        tap_grads
        + [jnp.concatenate([d_gain, ends], axis=1), jnp.zeros((3, HEAD_IN), F32)],
        axis=0,
    )

    @pl.when(head == pl.num_programs(0) - 1)
    def _():
        dv_ref[...] = grads_ref[:, : dv_ref.shape[1]].astype(BF16)


def mixer_specs(rows, wide):
    full = lambda shape: pl.BlockSpec(shape, lambda h: (0,) * len(shape))
    head_cols = pl.BlockSpec((rows, 2 * DK), lambda h: (0, h))
    scalars = pl.BlockSpec(memory_space=pltpu.SMEM)
    return [
        scalars, scalars, head_cols, head_cols, full((rows, wide)), full((rows, wide)),
        full((rows, 8)), full((8, rows)), pl.BlockSpec((KCONV, HEAD_IN), lambda h: (0, h)),
        full((1, DV)),
    ]


def padded_width(heads):
    return heads * 2 * DV + 128


def mixer_forward(args):
    pk, pv = args[2], args[4]
    rows, heads, wide = pk.shape[0], pk.shape[1] // (2 * DK), pv.shape[1]
    square = pl.BlockSpec((1, rows, rows), lambda h: (h, 0, 0))
    return pl.pallas_call(
        mixer_forward_kernel,
        grid=(heads,),
        in_specs=mixer_specs(rows, wide),
        out_specs=[pl.BlockSpec((rows, DV), lambda h: (0, h)), square],
        out_shape=[
            jax.ShapeDtypeStruct((rows, heads * DV), BF16),
            jax.ShapeDtypeStruct((heads, rows, rows), F32),
        ],
        scratch_shapes=[
            pltpu.VMEM((rows, padded_width(heads)), F32),
            pltpu.VMEM((rows, rows), F32),
        ],
        compiler_params=pltpu.CompilerParams(
            dimension_semantics=("arbitrary",), vmem_limit_bytes=50 * 2**20
        ),
        cost_estimate=pl.CostEstimate(
            flops=heads * 50 * 2 * rows**3, bytes_accessed=16 * 2**20, transcendentals=0
        ),
        name="mixer_forward",
    )(*args)


def mixer_backward(args, inverse, pg, rg):
    pk, pv = args[2], args[4]
    rows, heads, wide = pk.shape[0], pk.shape[1] // (2 * DK), pv.shape[1]
    square = pl.BlockSpec((1, rows, rows), lambda h: (h, 0, 0))
    head_cols = pl.BlockSpec((rows, DV), lambda h: (0, h))
    return pl.pallas_call(
        mixer_backward_kernel,
        grid=(heads,),
        in_specs=mixer_specs(rows, wide) + [square, head_cols, head_cols],
        out_specs=[
            pl.BlockSpec((rows, 2 * DK), lambda h: (0, h)),
            pl.BlockSpec((rows, wide), lambda h: (0, 0)),
            pl.BlockSpec((1, 8, HEAD_IN), lambda h: (h, 0, 0)),
        ],
        out_shape=[
            jax.ShapeDtypeStruct((rows, heads * 2 * DK), BF16),
            jax.ShapeDtypeStruct((rows, wide), BF16),
            jax.ShapeDtypeStruct((heads, 8, HEAD_IN), F32),
        ],
        scratch_shapes=[
            pltpu.VMEM((rows, padded_width(heads)), F32),
            pltpu.VMEM((rows, rows), F32),
            pltpu.VMEM((rows, padded_width(heads)), F32),
        ],
        compiler_params=pltpu.CompilerParams(
            dimension_semantics=("arbitrary",), vmem_limit_bytes=50 * 2**20
        ),
        cost_estimate=pl.CostEstimate(
            flops=heads * 50 * 2 * rows**3, bytes_accessed=20 * 2**20, transcendentals=0
        ),
        name="mixer_backward",
    )(*args, inverse, pg, rg)


def swap(value, axis):
    return lax.ppermute(value, axis, [(0, 1), (1, 0)])


def ring_order(n):
    if n == 8:
        return [0, 2, 4, 6, 7, 5, 3, 1]
    return list(range(n))


def ring_sum(parts, place, order):
    n = len(order)
    forward = [(order[i], order[(i + 1) % n]) for i in range(n)]
    backward = [(b, a) for a, b in forward]
    total = jnp.zeros(parts.shape, F32)

    def chunk(index, way):
        got = lax.dynamic_slice(parts, (index, way, 0, 0), (1, 1) + parts.shape[2:])
        return got.reshape(parts.shape[2:])

    held = [chunk(place, 0), chunk(place, 1)]
    for s in range(1, n):
        came = [lax.ppermute(held[0], "dp", forward), lax.ppermute(held[1], "dp", backward)]
        mine = [chunk((place - s) % n, 0), chunk((place + s) % n, 1)]
        held = [
            (came[w].astype(F32) + mine[w].astype(F32)).astype(BF16) for w in (0, 1)
        ]

    def put(total, value, index, way):
        return lax.dynamic_update_slice(
            total, value.astype(F32)[None, None], (index, way, 0, 0)
        )

    for s in range(n):
        total = put(total, held[0], (place + 1 - s) % n, 0)
        total = put(total, held[1], (place - 1 + s) % n, 1)
        if s < n - 1:
            held = [
                lax.ppermute(held[0], "dp", forward),
                lax.ppermute(held[1], "dp", backward),
            ]
    return total


def as_chunks(grad, n):
    return grad.reshape((n, 2, grad.shape[0] // (2 * n)) + grad.shape[1:])


def sum_groups(value, n):
    step = 1
    while step < n:
        value = value + lax.ppermute(value, "dp", [(i, i ^ step) for i in range(n)])
        step *= 2
    return value


def mm(a, b, dims=NN):
    return lax.dot_general(a, b, dims, preferred_element_type=F32)


def pair_sum(row_sums):
    return row_sums + swap(row_sums, "col")


def norm_forward(values, gain, width):
    totals = pair_sum(jnp.sum(values * values, axis=1))
    scale = lax.rsqrt(totals / width + 1e-05)
    return (values * scale[:, None] * gain[None, :]).astype(BF16), scale


def norm_backward(values, gain, scale, grad, width):
    scaled = grad * gain[None, :]
    inner = pair_sum(jnp.sum(scaled * values, axis=1))
    part = scale[:, None] * scaled - values * (scale * scale * scale * inner / width)[:, None]
    return part, jnp.sum(grad * values * scale[:, None], axis=0)


def layer(
    groups,
    inputs,
    gain_attn,
    w_keys,
    w_values,
    conv_weight,
    decay_log,
    step_bias,
    gain_head,
    w_out,
    gain_mlp,
    w_gate,
    w_up,
    w_down,
    seq_lens,
    cotangent,
):
    rows, half_width = inputs.shape
    width = 2 * half_width
    row = lax.axis_index("row")
    col = lax.axis_index("col")
    order = ring_order(groups)
    places = [0] * groups
    for i, d in enumerate(order):
        places[d] = i
    place = jnp.asarray(places, jnp.int32)[lax.axis_index("dp")]
    same = row == col

    def by_col(first, second):
        return jnp.where(same, first, second), jnp.where(same, second, first)

    ends = seq_lens[:, 0] + seq_lens[:, 1]
    positions = jnp.arange(rows, dtype=jnp.int32)
    row_mask = (positions < ends[row]).astype(F32)
    lens = seq_lens[col]
    segment = (positions >= lens[0]).astype(jnp.int32) + (
        positions >= lens[0] + lens[1]
    ).astype(jnp.int32)
    earlier = [
        ((jnp.roll(segment, s) == segment) & (positions >= s)).astype(F32)
        for s in range(1, KCONV)
    ]
    seg_f = segment.astype(F32)
    meta = jnp.stack([seg_f] + earlier + [seg_f] * (8 - KCONV), axis=1)
    seg_row = jnp.broadcast_to(seg_f[None, :], (8, rows))

    out_grad = cotangent * row_mask[:, None]
    mlp_grad_own = out_grad.astype(BF16)
    mlp_grad = jnp.concatenate([mlp_grad_own, swap(mlp_grad_own, "row")], axis=0)

    x = inputs.astype(F32)
    normed_own, scale_attn = norm_forward(x, gain_attn, width)
    normed_keep, normed_send = by_col(normed_own, swap(normed_own, "row"))
    rk = swap(mm(normed_send, w_keys).astype(BF16), "col")
    rv = swap(mm(normed_send, w_values).astype(BF16), "col")
    pk = mm(normed_keep, w_keys)
    pv = mm(normed_keep, w_values)
    mixer_args = (
        decay_log, step_bias, pk, rk, pv, rv, meta, seg_row, conv_weight, gain_head[None, :],
    )
    mixed_keep, inverse = mixer_forward(mixer_args)
    mixed_own, mixed_other = by_col(mixed_keep, swap(mixed_keep, "col"))

    hidden_part = mm(mlp_grad, w_down, NT)
    hidden_grad = hidden_part + swap(hidden_part.astype(BF16), "col").astype(F32)

    resid_mid = x + (mm(mixed_own, w_out) + swap(mm(mixed_other, w_out), "row"))

    normed_mlp_own, scale_mlp = norm_forward(resid_mid, gain_mlp, width)
    normed_mlp = jnp.concatenate([normed_mlp_own, swap(normed_mlp_own, "row")], axis=0)
    gate_part = mm(normed_mlp, w_gate)
    up_part = mm(normed_mlp, w_up)
    gate_pre = gate_part + swap(gate_part.astype(BF16), "col").astype(F32)
    up_pre = up_part + swap(up_part.astype(BF16), "col").astype(F32)
    sig = jax.nn.sigmoid(gate_pre)
    gate_act = gate_pre * sig
    hidden = (gate_act * up_pre).astype(BF16)
    gate_grad = (hidden_grad * up_pre * sig * (1.0 + gate_pre * (1.0 - sig))).astype(BF16)
    up_grad = (hidden_grad * gate_act).astype(BF16)

    normed_part = mm(gate_grad, w_gate, NT) + mm(up_grad, w_up, NT)
    normed_mlp_grad = normed_part[:rows] + swap(normed_part[rows:], "row")
    mid_grad, grad_gain_mlp = norm_backward(
        resid_mid, gain_mlp, scale_mlp, normed_mlp_grad, width
    )
    resid_grad = out_grad + mid_grad
    attn_grad_own = resid_grad.astype(BF16)
    attn_grad_other = swap(attn_grad_own, "row")
    attn_keep, attn_send = by_col(attn_grad_own, attn_grad_other)
    rg = swap(mm(attn_send, w_out, NT).astype(BF16), "col")
    pg = mm(attn_keep, w_out, NT)

    down_part = mm(hidden, w_down)
    result = resid_mid + (down_part[:rows] + swap(down_part[rows:], "row"))

    step = 16 * groups
    units = hidden.shape[1]
    padded = jnp.pad(hidden, ((0, 0), (0, -units % step)))
    grad_w_down = mm(padded, mlp_grad, TN).astype(BF16)
    grad_w_gate = mm(normed_mlp, gate_grad, TN).astype(BF16)
    grad_w_up = mm(normed_mlp, up_grad, TN).astype(BF16)
    mixed_rows = jnp.concatenate([mixed_own, mixed_other], axis=0)
    attn_rows = jnp.concatenate([attn_grad_own, attn_grad_other], axis=0)
    grad_w_out = mm(mixed_rows, attn_rows, TN).astype(BF16)

    def reduced(grad):
        total = ring_sum(as_chunks(grad, groups), place, order)
        return total.reshape(grad.shape)

    grad_w_down = reduced(grad_w_down)[:units]
    grad_w_gate = reduced(grad_w_gate)
    grad_w_up = reduced(grad_w_up)
    grad_w_out = reduced(grad_w_out)

    dk_keep, dv_keep, small = mixer_backward(mixer_args, inverse, pg, rg)
    dk_send, dv_send = swap(dk_keep, "col"), swap(dv_keep, "col")
    normed_rows = jnp.concatenate([normed_keep, normed_send], axis=0)
    dk = jnp.concatenate([dk_keep, dk_send], axis=0)
    dv = jnp.concatenate([dv_keep, dv_send], axis=0)
    grad_w_keys = reduced(mm(normed_rows, dk, TN).astype(BF16))
    grad_w_values = reduced(mm(normed_rows, dv, TN).astype(BF16))
    back = mm(dk, w_keys, NT) + mm(dv, w_values, NT)
    back_own, back_other = by_col(back[:rows], back[rows:])
    normed_attn_grad = back_own + swap(back_other, "row")
    input_part, grad_gain_attn = norm_backward(
        x, gain_attn, scale_attn, normed_attn_grad, width
    )
    input_grad = resid_grad + input_part

    heads = small.shape[0]
    taps = small[:, :KCONV]
    others = small[:, KCONV]
    gain_row = jnp.pad(jnp.sum(others[:, :DV], axis=0), (0, HEAD_IN - DV))
    gain_row = gain_row + swap(gain_row, "row")
    ends_row = jnp.pad(others[:, DV : DV + 2].reshape(-1), (0, HEAD_IN - 2 * heads))
    by_col_sums = jnp.concatenate(
        [taps.reshape(-1, HEAD_IN), gain_row[None], ends_row[None]], axis=0
    )
    by_col_sums = by_col_sums + swap(by_col_sums, "col")
    gains = jnp.concatenate([grad_gain_attn, grad_gain_mlp]).reshape(-1, HEAD_IN)
    gains = gains + swap(gains, "row")
    sums = sum_groups(jnp.concatenate([by_col_sums, gains], axis=0), groups)
    tap_rows = heads * KCONV
    grad_conv = jnp.swapaxes(
        sums[:tap_rows].reshape(heads, KCONV, HEAD_IN), 0, 1
    ).reshape(KCONV, heads * HEAD_IN)
    grad_gain_head = sums[tap_rows, :DV]
    end_pairs = sums[tap_rows + 1, : 2 * heads].reshape(heads, 2)
    gain_sums = sums[tap_rows + 2 :].reshape(2, half_width)
    return (
        result,
        input_grad,
        gain_sums[0],
        grad_w_keys,
        grad_w_values,
        grad_conv,
        end_pairs[:, 0],
        end_pairs[:, 1],
        grad_gain_head,
        grad_w_out,
        gain_sums[1],
        grad_w_gate,
        grad_w_up,
        grad_w_down,
    )


def solution(mesh):
    tokens, weights, back = P(("dp", "row"), "col"), P("col", "row"), P("row", "col")
    in_specs = (
        tokens, P("col"), weights, weights, P(None, "row"), P("row"), P("row"), P(), back,
        P("col"), weights, weights, back, P("dp", None), tokens,
    )
    out_specs = (
        tokens, tokens, P("col"), weights, weights, P(None, "row"), P("row"), P("row"), P(),
        back, P("col"), weights, weights, back,
    )
    return jax.shard_map(
        partial(layer, mesh.shape["dp"]),
        mesh=mesh,
        in_specs=in_specs,
        out_specs=out_specs,
        check_vma=False,
    )
```

time: 3410 us -> 1300 us (0.38)
  waiting for transfers between devices: 2560 us -> 522 us
  starting transfers between devices: 1.78 us -> 221 us
  matrix products: 272 us -> 114 us
  other arithmetic: 294 us -> 180 us
  blocking collectives: 105 us -> 0 us
  Pallas kernels: 0 us -> 97.7 us
    psum x1 -> x0, waiting for transfers between devices: 1910 us -> none  [shards(): lax.psum((grad_w_keys, grad_w_values, grad_conv, grad_decay_log, grad_ste...]
    ppermute x0 -> x195, waiting for transfers between devices: none -> 522 us  [the longest x24 234 us: swap(): return lax.ppermute(value, axis, [(0, 1), (1, 0)])]
    reduce_scatter x8 -> x0, waiting for transfers between devices: 393 us -> none  [the longest x2 272 us: project_in(): lax.psum_scatter(rows_pair(normed_rows, first_w, second_w), 'col', scatte...]
    all_gather x10 -> x0, waiting for transfers between devices: 251 us -> none  [the longest x2 89.5 us: project_back(): lax.all_gather(second_grad, 'col', axis=0, tiled=True)]
    ppermute x0 -> x195, starting transfers between devices: none -> 221 us  [the longest x84 112 us: ring_sum(): lax.ppermute(held[0], 'dp', forward)]
    another operation x8 -> x0, other arithmetic: 161 us -> none  [the longest x3 158 us: delta_mixer(): jax.scipy.linalg.solve_triangular(system, right_side, lower=True, unit_di...]
    dot_general x73 -> x22, matrix products: 258 us -> 114 us  [mm(): return lax.dot_general(a, b, dims, preferred_element_type=F32)]
    psum x7 -> x0, blocking collectives: 105 us -> none  [the longest x1 43.1 us: shards(): lax.psum((grad_w_keys, grad_w_values, grad_conv, grad_decay_log, grad_ste...]
  transfers between devices with their start and end apart: 19 -> 195, of which waited for: 18 -> 98; matrix products, arithmetic and copies ran while one was open for 4% -> 29% of each run, Pallas kernels for 0% -> 3%
where the time goes in v1:
time: 1300 us; the launch traced here: 1290 us
  waiting for transfers between devices  522 us (40%)
  starting transfers between devices  221 us (17%)
  other arithmetic  180 us (14%)
  local copies, waits for them, and re-layouts  143 us (11%)
  matrix products  114 us (9%)
  Pallas kernels  97.7 us (8%)
  between operations  16.2 us (1%)
    ppermute x24, waiting for transfers between devices, swap(): return lax.ppermute(value, axis, [(0, 1), (1, 0)])  234 us
    ppermute x84, waiting for transfers between devices, ring_sum(): lax.ppermute(held[0], 'dp', forward)  184 us
    dot_general x22, matrix products, mm(): return lax.dot_general(a, b, dims, preferred_element_type=F32)  114 us
    dynamic_update_slice x96, other arithmetic, put(): lax.dynamic_update_slice(total, value.astype(F32)[None, None], (index, wa...  113 us
    ppermute x84, starting transfers between devices, ring_sum(): lax.ppermute(held[0], 'dp', forward)  112 us
    ppermute x84, waiting for transfers between devices, ring_sum(): lax.ppermute(held[1], 'dp', backward)  99 us
    ppermute x84, starting transfers between devices, ring_sum(): lax.ppermute(held[1], 'dp', backward)  83.7 us
    pallas_call x1, Pallas kernels, mixer_forward(): pl.pallas_call(mixer_forward_kernel, grid=(heads,), in_specs=mixer_specs(...  56.1 us
  transfers between devices with their start and end apart: 195, of which 98 were waited for; matrix products, arithmetic and copies ran while one was open for 29% of the time, Pallas kernels for 3%

profile of v1, /device:TPU:0, one launch (start us, length us, event | category | flops | bytes accessed | tf_op | source)
XLA Modules:
  0.0 1294.2 jit_solution(18142075791582472829)
XLA Ops:
  13.3 7.3 convolution_convert_fusion.1
  36.2 8.2 fusion.146.pv_ref
  44.4 25.1 %collective-permute-done.3 = bf16[256,4112]{0,1:T(8,128)(2,1)S(1)} collective-permute-done((bf16[256,4112]{0,1:T(8,128)(2,1)}, bf16[256,4112]{0,1:T(8,128)(2,1)S(1)}, u32[]{:S(2)}, u32[]{:S(2)}) %collective-permute-start.3) | collective-permute-done | bytes 2105376 | tf_op jit(solution)/shard_map/ppermute | solution.py:345
  72.6 19.1 %collective-permute-done.2.rk_ref = bf16[256,2048]{1,0:T(8,128)(2,1)S(1)} collective-permute-done((bf16[256,2048]{1,0:T(8,128)(2,1)}, bf16[256,2048]{1,0:T(8,128)(2,1)S(1)}, u32[]{:S(2)}, u32[]{:S(2)}) %collective-permute-start.2) | collective-permute-done | bytes 1048608 | tf_op jit(solution)/shard_map/ppermute | solution.py:345
  91.8 56.1 %mixer_forward.1 = (bf16[256,2048]{1,0:T(8,128)(2,1)S(1)}, f32[8,256,256]{2,1,0:T(8,128)}) custom-call(f32[8]{0:T(128)S(1)} %copy-done.2, f32[8]{0:T(128)S(1)} %copy-done.3, f32[256,2048]{1,0:T(8,128)} %fusion.145.pk_ref, bf16[256,2048]{1,0:T(8,128)(2,1)S(1)} %collective-permute-done.2.rk_ref, f32[256,4112]{1,0:T(8,128)} %fusion.146.pv_ref, ...), custom_call_target="tpu_custom_call" | custom-call | flops 13421772800 | bytes 16777216 | tf_op jit(solution)/shard_map/mixer_forward/pallas_call | solution.py:287
  149.7 23.2 %collective-permute-done.4 = bf16[256,2048]{1,0:T(8,128)(2,1)S(1)} collective-permute-done((bf16[256,2048]{1,0:T(8,128)(2,1)S(1)}, bf16[256,2048]{1,0:T(8,128)(2,1)S(1)}, u32[]{:S(2)}, u32[]{:S(2)}) %collective-permute-start.4) | collective-permute-done | bytes 1048608 | tf_op jit(solution)/shard_map/ppermute | solution.py:345
  187.4 8.9 fusion.141
  198.0 5.3 fusion.142
  203.8 5.7 fusion.143
  224.2 36.4 %collective-permute-done.12 = bf16[512,2752]{0,1:T(8,128)(2,1)} collective-permute-done((bf16[512,2752]{0,1:T(8,128)(2,1)}, bf16[512,2752]{0,1:T(8,128)(2,1)}, u32[]{:S(2)}, u32[]{:S(2)}) %collective-permute-start.12) | collective-permute-done | bytes 2818080 | tf_op jit(solution)/shard_map/ppermute | solution.py:345
  260.6 60.4 %collective-permute-done.8 = bf16[512,2752]{0,1:T(8,128)(2,1)} collective-permute-done((bf16[512,2752]{0,1:T(8,128)(2,1)}, bf16[512,2752]{0,1:T(8,128)(2,1)}, u32[]{:S(2)}, u32[]{:S(2)}) %collective-permute-start.8) | collective-permute-done | bytes 2818080 | tf_op jit(solution)/shard_map/ppermute | solution.py:345
  321.0 59.6 %collective-permute-done.9 = bf16[512,2752]{0,1:T(8,128)(2,1)} collective-permute-done((bf16[512,2752]{0,1:T(8,128)(2,1)}, bf16[512,2752]{0,1:T(8,128)(2,1)}, u32[]{:S(2)}, u32[]{:S(2)}) %collective-permute-start.9) | collective-permute-done | bytes 2818080 | tf_op jit(solution)/shard_map/ppermute | solution.py:345
  380.6 10.1 multiply_convert_fusion
  390.8 7.3 fusion.149
  398.1 5.3 fusion.144
  415.1 8.3 copy.145
  427.6 7.6 convolution_convert_fusion.2
  435.3 8.3 copy.146
  446.8 5.2 convolution_convert_fusion.4
  548.9 12.2 collective-permute-done.90
  567.2 5.2 collective-permute-done.171
  616.2 5.6 broadcast.130.clone
  624.3 5.4 broadcast.130.clone.1
  637.9 5.8 broadcast_in_dim.783
  646.4 41.6 %mixer_backward.1 = (bf16[256,2048]{1,0:T(8,128)(2,1)S(1)}, bf16[256,4112]{1,0:T(8,128)(2,1)}, f32[8,8,512]{2,1,0:T(8,128)S(1)}) custom-call(f32[8]{0:T(128)S(1)} %copy-done.2, f32[8]{0:T(128)S(1)} %copy-done.3, f32[256,2048]{1,0:T(8,128)} %fusion.145.pk_ref, bf16[256,2048]{1,0:T(8,128)(2,1)S(1)} %collective-permute-done.2.rk_ref, ...), custom_call_target="tpu_custom_call" | custom-call | flops 13421772800 | bytes 20971520 | tf_op jit(solution)/shard_map/mixer_backward/pallas_call | solution.py:315
  709.4 10.0 collective-permute-done.94
  814.4 7.1 collective-permute-done.34
  823.8 7.1 collective-permute-done.99
  926.2 10.3 fusion.2
  936.5 6.8 convolution_convert_fusion
  947.3 11.6 copy.143
  973.8 11.8 copy.148
  985.6 11.8 copy.149
  1013.8 11.0 slice.139
  1028.3 5.3 collective-permute-done.109
  1092.6 5.3 collective-permute-done.45
  1111.0 11.9 collective-permute-done.49
  1132.8 6.8 collective-permute-done.66
  1149.4 7.3 collective-permute-done.67
  1162.0 6.7 collective-permute-done.61
  1168.8 7.7 broadcast_in_dim.653
  1183.3 8.2 collective-permute-done.69
  1196.8 7.2 collective-permute-done.71
  1209.4 7.5 collective-permute-done.73
  1222.7 8.6 collective-permute-done.75
  1237.0 9.5 collective-permute-done.77
  1252.1 9.2 collective-permute-done.79
  1275.8 18.0 %copy.147 = f32[1024,4112]{0,1:T(8,128)} copy(f32[1024,4112]{1,0:T(8,128)} %bitcast.80) | data formatting | bytes 33685504
  (706 shorter events, 628.0 us)
Async XLA Ops:
  20.6 48.9 %collective-permute-start.3 = (bf16[256,4112]{0,1:T(8,128)(2,1)}, bf16[256,4112]{0,1:T(8,128)(2,1)S(1)}, u32[]{:S(2)}, u32[]{:S(2)}) collective-permute-start(bf16[256,4112]{0,1:T(8,128)(2,1)} %convolution_convert_fusion.1), channel_id=1, source_target_pairs={{0,1},{1,0},{2,3},{3,2},{4,5},{5,4},{6,7},{7,6},{8,9},{9,8},{10,11... | collective-permute-start | bytes 6316040 | tf_op jit(solution)/shard_map/ppermute | solution.py:345
  31.2 60.5 %collective-permute-start.2 = (bf16[256,2048]{1,0:T(8,128)(2,1)}, bf16[256,2048]{1,0:T(8,128)(2,1)S(1)}, u32[]{:S(2)}, u32[]{:S(2)}) collective-permute-start(bf16[256,2048]{1,0:T(8,128)(2,1)} %convolution_convert_fusion.8), channel_id=1, source_target_pairs={{0,1},{1,0},{2,3},{3,2},{4,5},{5,4},{6,7},{7,6},{8,9},{9,8},{10,11... | collective-permute-start | bytes 3145736 | tf_op jit(solution)/shard_map/ppermute | solution.py:345
  147.9 25.1 %collective-permute-start.4 = (bf16[256,2048]{1,0:T(8,128)(2,1)S(1)}, bf16[256,2048]{1,0:T(8,128)(2,1)S(1)}, u32[]{:S(2)}, u32[]{:S(2)}) collective-permute-start(bf16[256,2048]{1,0:T(8,128)(2,1)S(1)} %get-tuple-element.19), channel_id=1, source_target_pairs={{0,1},{1,0},{2,3},{3,2},{4,5},{5,4},{6,7},{7,6},{8,9},{9,8},{10,11... | collective-permute-start | bytes 3145736 | tf_op jit(solution)/shard_map/ppermute | solution.py:345
  196.3 64.3 %collective-permute-start.12 = (bf16[512,2752]{0,1:T(8,128)(2,1)}, bf16[512,2752]{0,1:T(8,128)(2,1)}, u32[]{:S(2)}, u32[]{:S(2)}) collective-permute-start(bf16[512,2752]{0,1:T(8,128)(2,1)} %get-tuple-element.183), channel_id=1, source_target_pairs={{0,1},{1,0},{2,3},{3,2},{4,5},{5,4},{6,7},{7,6},{8,9},{9,8},{10,11... | collective-permute-start | bytes 8454152 | tf_op jit(solution)/shard_map/ppermute | solution.py:345
  203.3 117.8 %collective-permute-start.8 = (bf16[512,2752]{0,1:T(8,128)(2,1)}, bf16[512,2752]{0,1:T(8,128)(2,1)}, u32[]{:S(2)}, u32[]{:S(2)}) collective-permute-start(bf16[512,2752]{0,1:T(8,128)(2,1)} %get-tuple-element.185), channel_id=1, source_target_pairs={{0,1},{1,0},{2,3},{3,2},{4,5},{5,4},{6,7},{7,6},{8,9},{9,8},{10,11... | collective-permute-start | bytes 8454152 | tf_op jit(solution)/shard_map/ppermute | solution.py:345
  209.5 171.1 %collective-permute-start.9 = (bf16[512,2752]{0,1:T(8,128)(2,1)}, bf16[512,2752]{0,1:T(8,128)(2,1)}, u32[]{:S(2)}, u32[]{:S(2)}) collective-permute-start(bf16[512,2752]{0,1:T(8,128)(2,1)} %get-tuple-element.187), channel_id=1, source_target_pairs={{0,1},{1,0},{2,3},{3,2},{4,5},{5,4},{6,7},{7,6},{8,9},{9,8},{10,11... | collective-permute-start | bytes 8454152 | tf_op jit(solution)/shard_map/ppermute | solution.py:345
  404.6 79.2 %collective-permute-start.13 = (f32[256,1024]{1,0:T(8,128)}, f32[256,1024]{1,0:T(8,128)}, u32[]{:S(2)}, u32[]{:S(2)}) collective-permute-start(f32[256,1024]{1,0:T(8,128)} %slice.129), channel_id=1, source_target_pairs={{0,2},{2,0},{1,3},{3,1},{4,6},{6,4},{5,7},{7,5},{8,10},{10,8},{9,1... | collective-permute-start | bytes 3145736 | tf_op jit(solution)/shard_map/ppermute | solution.py:345
  425.4 26.7 %collective-permute-start.118 = (bf16[64,2752]{1,0:T(8,128)(2,1)}, bf16[64,2752]{1,0:T(8,128)(2,1)}, u32[]{:S(2)}, u32[]{:S(2)}) collective-permute-start(bf16[64,2752]{1,0:T(8,128)(2,1)} %get-tuple-element.142), channel_id=1, source_target_pairs={{8,0},{16,8},{24,16},{28,24},{20,28},{12,20},{4,12},{0,4},{9,1},{1... | collective-permute-start | bytes 1056776 | tf_op jit(solution)/shard_map/ppermute | solution.py:366
  427.0 26.7 %collective-permute-start.111 = (bf16[64,2752]{1,0:T(8,128)(2,1)}, bf16[64,2752]{1,0:T(8,128)(2,1)}, u32[]{:S(2)}, u32[]{:S(2)}) collective-permute-start(bf16[64,2752]{1,0:T(8,128)(2,1)} %get-tuple-element.143), channel_id=1, source_target_pairs={{0,8},{8,16},{16,24},{24,28},{28,20},{20,12},{12,4},{4,0},{1,9},{9... | collective-permute-start | bytes 1056776 | tf_op jit(solution)/shard_map/ppermute | solution.py:366
  463.6 32.0 %collective-permute-start.10 = (f32[256,1024]{1,0:T(8,128)}, f32[256,1024]{1,0:T(8,128)}, u32[]{:S(2)}, u32[]{:S(2)}) collective-permute-start(f32[256,1024]{1,0:T(8,128)} %slice.127), channel_id=1, source_target_pairs={{0,2},{2,0},{1,3},{3,1},{4,6},{6,4},{5,7},{7,5},{8,10},{10,8},{9,1... | collective-permute-start | bytes 3145736 | tf_op jit(solution)/shard_map/ppermute | solution.py:345
  502.1 36.5 %collective-permute-start.15 = (bf16[256,1024]{1,0:T(8,128)(2,1)S(1)}, bf16[256,1024]{1,0:T(8,128)(2,1)S(1)}, u32[]{:S(2)}, u32[]{:S(2)}) collective-permute-start(bf16[256,1024]{1,0:T(8,128)(2,1)S(1)} %get-tuple-element.83), channel_id=1, source_target_pairs={{0,2},{2,0},{1,3},{3,1},{4,6},{6,4},{5,7},{7,5},{8,10},{10,8},{9,1... | collective-permute-start | bytes 1572872 | tf_op jit(solution)/shard_map/ppermute | solution.py:345
  533.1 31.3 %collective-permute-start.150 = (bf16[64,2752]{1,0:T(8,128)(2,1)S(1)}, bf16[64,2752]{1,0:T(8,128)(2,1)S(1)}, u32[]{:S(2)}, u32[]{:S(2)}) collective-permute-start(bf16[64,2752]{1,0:T(8,128)(2,1)S(1)} %get-tuple-element.120), channel_id=1, source_target_pairs={{8,0},{16,8},{24,16},{28,24},{20,28},{12,20},{4,12},{0,4},{9,1},{1... | collective-permute-start | bytes 1056776 | tf_op jit(solution)/shard_map/ppermute | solution.py:366
  536.7 28.2 %collective-permute-start.143 = (bf16[64,2752]{1,0:T(8,128)(2,1)S(1)}, bf16[64,2752]{1,0:T(8,128)(2,1)S(1)}, u32[]{:S(2)}, u32[]{:S(2)}) collective-permute-start(bf16[64,2752]{1,0:T(8,128)(2,1)S(1)} %get-tuple-element.121), channel_id=1, source_target_pairs={{0,8},{8,16},{16,24},{24,28},{28,20},{20,12},{12,4},{4,0},{1,9},{9... | collective-permute-start | bytes 1056776 | tf_op jit(solution)/shard_map/ppermute | solution.py:366
  538.6 28.0 %collective-permute-start.178 = (bf16[176,1024]{1,0:T(8,128)(2,1)S(1)}, bf16[176,1024]{1,0:T(8,128)(2,1)S(1)}, u32[]{:S(2)}, u32[]{:S(2)}) collective-permute-start(bf16[176,1024]{1,0:T(8,128)(2,1)S(1)} %get-tuple-element.106), channel_id=1, source_target_pairs={{8,0},{16,8},{24,16},{28,24},{20,28},{12,20},{4,12},{0,4},{9,1},{1... | collective-permute-start | bytes 1081352 | tf_op jit(solution)/shard_map/ppermute | solution.py:366
  562.7 83.7 %collective-permute-start.16 = (bf16[256,2048]{1,0:T(8,128)(2,1)S(1)}, bf16[256,2048]{1,0:T(8,128)(2,1)S(1)}, u32[]{:S(2)}, u32[]{:S(2)}) collective-permute-start(bf16[256,2048]{1,0:T(8,128)(2,1)S(1)} %convolution_convert_fusion.7), channel_id=1, source_target_pairs={{0,1},{1,0},{2,3},{3,2},{4,5},{5,4},{6,7},{7,6},{8,9},{9,8},{10,11... | collective-permute-start | bytes 3145736 | tf_op jit(solution)/shard_map/ppermute | solution.py:345
  601.2 29.5 %collective-permute-start.124 = (bf16[64,2752]{1,0:T(8,128)(2,1)S(1)}, bf16[64,2752]{1,0:T(8,128)(2,1)S(1)}, u32[]{:S(2)}, u32[]{:S(2)}) collective-permute-start(bf16[64,2752]{1,0:T(8,128)(2,1)S(1)} %get-tuple-element.130), channel_id=1, source_target_pairs={{8,0},{16,8},{24,16},{28,24},{20,28},{12,20},{4,12},{0,4},{9,1},{1... | collective-permute-start | bytes 1056776 | tf_op jit(solution)/shard_map/ppermute | solution.py:366
  606.8 27.5 %collective-permute-start.152 = (bf16[64,2752]{1,0:T(8,128)(2,1)S(1)}, bf16[64,2752]{1,0:T(8,128)(2,1)S(1)}, u32[]{:S(2)}, u32[]{:S(2)}) collective-permute-start(bf16[64,2752]{1,0:T(8,128)(2,1)S(1)} %get-tuple-element.116), channel_id=1, source_target_pairs={{8,0},{16,8},{24,16},{28,24},{20,28},{12,20},{4,12},{0,4},{9,1},{1... | collective-permute-start | bytes 1056776 | tf_op jit(solution)/shard_map/ppermute | solution.py:366
  614.5 21.3 %collective-permute-start.173 = (bf16[176,1024]{1,0:T(8,128)(2,1)S(1)}, bf16[176,1024]{1,0:T(8,128)(2,1)S(1)}, u32[]{:S(2)}, u32[]{:S(2)}) collective-permute-start(bf16[176,1024]{1,0:T(8,128)(2,1)S(1)} %get-tuple-element.103), channel_id=1, source_target_pairs={{0,8},{8,16},{16,24},{24,28},{28,20},{20,12},{12,4},{4,0},{1,9},{9... | collective-permute-start | bytes 1081352 | tf_op jit(solution)/shard_map/ppermute | solution.py:366
  630.7 64.6 %collective-permute-start.93 = (bf16[128,1024]{1,0:T(8,128)(2,1)}, bf16[128,1024]{1,0:T(8,128)(2,1)}, u32[]{:S(2)}, u32[]{:S(2)}) collective-permute-start(bf16[128,1024]{1,0:T(8,128)(2,1)} %get-tuple-element.150), channel_id=1, source_target_pairs={{8,0},{16,8},{24,16},{28,24},{20,28},{12,20},{4,12},{0,4},{9,1},{1... | collective-permute-start | bytes 786440 | tf_op jit(solution)/shard_map/ppermute | solution.py:366
  634.4 61.3 %collective-permute-start.86 = (bf16[128,1024]{1,0:T(8,128)(2,1)}, bf16[128,1024]{1,0:T(8,128)(2,1)}, u32[]{:S(2)}, u32[]{:S(2)}) collective-permute-start(bf16[128,1024]{1,0:T(8,128)(2,1)} %get-tuple-element.151), channel_id=1, source_target_pairs={{0,8},{8,16},{16,24},{24,28},{28,20},{20,12},{12,4},{4,0},{1,9},{9... | collective-permute-start | bytes 786440 | tf_op jit(solution)/shard_map/ppermute | solution.py:366
  635.9 66.0 %collective-permute-start.125 = (bf16[64,2752]{1,0:T(8,128)(2,1)}, bf16[64,2752]{1,0:T(8,128)(2,1)S(1)}, u32[]{:S(2)}, u32[]{:S(2)}) collective-permute-start(bf16[64,2752]{1,0:T(8,128)(2,1)} %get-tuple-element.69), channel_id=1, source_target_pairs={{0,8},{8,16},{16,24},{24,28},{28,20},{20,12},{12,4},{4,0},{1,9},{9... | collective-permute-start | bytes 1056776 | tf_op jit(solution)/shard_map/ppermute | solution.py:382
  644.9 58.2 %collective-permute-start.126 = (bf16[64,2752]{1,0:T(8,128)(2,1)}, bf16[64,2752]{1,0:T(8,128)(2,1)S(1)}, u32[]{:S(2)}, u32[]{:S(2)}) collective-permute-start(bf16[64,2752]{1,0:T(8,128)(2,1)} %get-tuple-element.67), channel_id=1, source_target_pairs={{8,0},{16,8},{24,16},{28,24},{20,28},{12,20},{4,12},{0,4},{9,1},{1... | collective-permute-start | bytes 1056776 | tf_op jit(solution)/shard_map/ppermute | solution.py:383
  700.1 22.4 %collective-permute-start.181 = (bf16[176,1024]{1,0:T(8,128)(2,1)S(1)}, bf16[176,1024]{1,0:T(8,128)(2,1)S(1)}, u32[]{:S(2)}, u32[]{:S(2)}) collective-permute-start(bf16[176,1024]{1,0:T(8,128)(2,1)S(1)} %copy-done.35), channel_id=1, source_target_pairs={{0,8},{8,16},{16,24},{24,28},{28,20},{20,12},{12,4},{4,0},{1,9},{9... | collective-permute-start | bytes 1081352 | tf_op jit(solution)/shard_map/ppermute | solution.py:382
  701.9 23.3 %collective-permute-start.182 = (bf16[176,1024]{1,0:T(8,128)(2,1)S(1)}, bf16[176,1024]{1,0:T(8,128)(2,1)S(1)}, u32[]{:S(2)}, u32[]{:S(2)}) collective-permute-start(bf16[176,1024]{1,0:T(8,128)(2,1)S(1)} %copy-done.36), channel_id=1, source_target_pairs={{8,0},{16,8},{24,16},{28,24},{20,28},{12,20},{4,12},{0,4},{9,1},{1... | collective-permute-start | bytes 1081352 | tf_op jit(solution)/shard_map/ppermute | solution.py:383
  703.1 89.4 %collective-permute-start.17 = (bf16[256,2048]{1,0:T(8,128)(2,1)S(1)}, bf16[256,2048]{1,0:T(8,128)(2,1)S(1)}, u32[]{:S(2)}, u32[]{:S(2)}) collective-permute-start(bf16[256,2048]{1,0:T(8,128)(2,1)S(1)} %get-tuple-element.21), channel_id=1, source_target_pairs={{0,1},{1,0},{2,3},{3,2},{4,5},{5,4},{6,7},{7,6},{8,9},{9,8},{10,11... | collective-permute-start | bytes 3145736 | tf_op jit(solution)/shard_map/ppermute | solution.py:345
  719.4 201.3 %collective-permute-start.18 = (bf16[256,4112]{0,1:T(8,128)(2,1)}, bf16[256,4112]{0,1:T(8,128)(2,1)}, u32[]{:S(2)}, u32[]{:S(2)}) collective-permute-start(bf16[256,4112]{0,1:T(8,128)(2,1)} %copy.141), channel_id=1, source_target_pairs={{0,1},{1,0},{2,3},{3,2},{4,5},{5,4},{6,7},{7,6},{8,9},{9,8},{10,11... | collective-permute-start | bytes 6316040 | tf_op jit(solution)/shard_map/ppermute | solution.py:345
  802.1 32.5 %collective-permute-start.187 = (bf16[176,1024]{1,0:T(8,128)(2,1)S(1)}, bf16[176,1024]{1,0:T(8,128)(2,1)S(1)}, u32[]{:S(2)}, u32[]{:S(2)}) collective-permute-start(bf16[176,1024]{1,0:T(8,128)(2,1)S(1)} %collective-permute-done.185), channel_id=1, source_target_pairs={{0,8},{8,16},{16,24},{24,28},{28,20},{20,12},{12,4},{4,0},{1,9},{9... | collective-permute-start | bytes 1081352 | tf_op jit(solution)/shard_map/ppermute | solution.py:382
  804.4 32.4 %collective-permute-start.188 = (bf16[176,1024]{1,0:T(8,128)(2,1)S(1)}, bf16[176,1024]{1,0:T(8,128)(2,1)S(1)}, u32[]{:S(2)}, u32[]{:S(2)}) collective-permute-start(bf16[176,1024]{1,0:T(8,128)(2,1)S(1)} %collective-permute-done.186), channel_id=1, source_target_pairs={{8,0},{16,8},{24,16},{28,24},{20,28},{12,20},{4,12},{0,4},{9,1},{1... | collective-permute-start | bytes 1081352 | tf_op jit(solution)/shard_map/ppermute | solution.py:383
  830.9 26.3 %collective-permute-start.133 = (bf16[64,2752]{1,0:T(8,128)(2,1)S(1)}, bf16[64,2752]{1,0:T(8,128)(2,1)S(1)}, u32[]{:S(2)}, u32[]{:S(2)}) collective-permute-start(bf16[64,2752]{1,0:T(8,128)(2,1)S(1)} %collective-permute-done.131), channel_id=1, source_target_pairs={{0,8},{8,16},{16,24},{24,28},{28,20},{20,12},{12,4},{4,0},{1,9},{9... | collective-permute-start | bytes 1056776 | tf_op jit(solution)/shard_map/ppermute | solution.py:382
  836.8 21.3 %collective-permute-start.134 = (bf16[64,2752]{1,0:T(8,128)(2,1)S(1)}, bf16[64,2752]{1,0:T(8,128)(2,1)S(1)}, u32[]{:S(2)}, u32[]{:S(2)}) collective-permute-start(bf16[64,2752]{1,0:T(8,128)(2,1)S(1)} %collective-permute-done.132), channel_id=1, source_target_pairs={{8,0},{16,8},{24,16},{28,24},{20,28},{12,20},{4,12},{0,4},{9,1},{1... | collective-permute-start | bytes 1056776 | tf_op jit(solution)/shard_map/ppermute | solution.py:383
  913.3 48.9 %collective-permute-start.137 = (bf16[64,2752]{1,0:T(8,128)(2,1)}, bf16[64,2752]{1,0:T(8,128)(2,1)}, u32[]{:S(2)}, u32[]{:S(2)}) collective-permute-start(bf16[64,2752]{1,0:T(8,128)(2,1)} %collective-permute-done.135), channel_id=1, source_target_pairs={{0,8},{8,16},{16,24},{24,28},{28,20},{20,12},{12,4},{4,0},{1,9},{9... | collective-permute-start | bytes 1056776 | tf_op jit(solution)/shard_map/ppermute | solution.py:382
  914.6 50.3 %collective-permute-start.138 = (bf16[64,2752]{1,0:T(8,128)(2,1)}, bf16[64,2752]{1,0:T(8,128)(2,1)}, u32[]{:S(2)}, u32[]{:S(2)}) collective-permute-start(bf16[64,2752]{1,0:T(8,128)(2,1)} %collective-permute-done.136), channel_id=1, source_target_pairs={{8,0},{16,8},{24,16},{28,24},{20,28},{12,20},{4,12},{0,4},{9,1},{1... | collective-permute-start | bytes 1056776 | tf_op jit(solution)/shard_map/ppermute | solution.py:383
  917.0 51.3 %collective-permute-start.165 = (bf16[64,2752]{1,0:T(8,128)(2,1)}, bf16[64,2752]{1,0:T(8,128)(2,1)}, u32[]{:S(2)}, u32[]{:S(2)}) collective-permute-start(bf16[64,2752]{1,0:T(8,128)(2,1)} %collective-permute-done.163), channel_id=1, source_target_pairs={{0,8},{8,16},{16,24},{24,28},{28,20},{20,12},{12,4},{4,0},{1,9},{9... | collective-permute-start | bytes 1056776 | tf_op jit(solution)/shard_map/ppermute | solution.py:382
  919.1 51.7 %collective-permute-start.166 = (bf16[64,2752]{1,0:T(8,128)(2,1)}, bf16[64,2752]{1,0:T(8,128)(2,1)}, u32[]{:S(2)}, u32[]{:S(2)}) collective-permute-start(bf16[64,2752]{1,0:T(8,128)(2,1)} %collective-permute-done.164), channel_id=1, source_target_pairs={{8,0},{16,8},{24,16},{28,24},{20,28},{12,20},{4,12},{0,4},{9,1},{1... | collective-permute-start | bytes 1056776 | tf_op jit(solution)/shard_map/ppermute | solution.py:383
  920.8 85.4 %collective-permute-start.193 = (bf16[176,1024]{1,0:T(8,128)(2,1)}, bf16[176,1024]{1,0:T(8,128)(2,1)}, u32[]{:S(2)}, u32[]{:S(2)}) collective-permute-start(bf16[176,1024]{1,0:T(8,128)(2,1)} %collective-permute-done.191), channel_id=1, source_target_pairs={{0,8},{8,16},{16,24},{24,28},{28,20},{20,12},{12,4},{4,0},{1,9},{9... | collective-permute-start | bytes 1081352 | tf_op jit(solution)/shard_map/ppermute | solution.py:382
  962.1 47.6 %collective-permute-start.194 = (bf16[176,1024]{1,0:T(8,128)(2,1)S(1)}, bf16[176,1024]{1,0:T(8,128)(2,1)}, u32[]{:S(2)}, u32[]{:S(2)}) collective-permute-start(bf16[176,1024]{1,0:T(8,128)(2,1)S(1)} %copy-done.34), channel_id=1, source_target_pairs={{8,0},{16,8},{24,16},{28,24},{20,28},{12,20},{4,12},{0,4},{9,1},{1... | collective-permute-start | bytes 1081352 | tf_op jit(solution)/shard_map/ppermute | solution.py:383
  964.9 32.6 %collective-permute-start.38 = (bf16[64,2048]{1,0:T(8,128)(2,1)}, bf16[64,2048]{1,0:T(8,128)(2,1)}, u32[]{:S(2)}, u32[]{:S(2)}) collective-permute-start(bf16[64,2048]{1,0:T(8,128)(2,1)} %get-tuple-element.162), channel_id=1, source_target_pairs={{8,0},{16,8},{24,16},{28,24},{20,28},{12,20},{4,12},{0,4},{9,1},{1... | collective-permute-start | bytes 786440 | tf_op jit(solution)/shard_map/ppermute | solution.py:366
  968.4 30.0 %collective-permute-start.31 = (bf16[64,2048]{1,0:T(8,128)(2,1)}, bf16[64,2048]{1,0:T(8,128)(2,1)}, u32[]{:S(2)}, u32[]{:S(2)}) collective-permute-start(bf16[64,2048]{1,0:T(8,128)(2,1)} %get-tuple-element.163), channel_id=1, source_target_pairs={{0,8},{8,16},{16,24},{24,28},{28,20},{20,12},{12,4},{4,0},{1,9},{9... | collective-permute-start | bytes 786440 | tf_op jit(solution)/shard_map/ppermute | solution.py:366
  970.7 28.9 %collective-permute-start.107 = (bf16[128,1024]{1,0:T(8,128)(2,1)S(1)}, bf16[128,1024]{1,0:T(8,128)(2,1)}, u32[]{:S(2)}, u32[]{:S(2)}) collective-permute-start(bf16[128,1024]{1,0:T(8,128)(2,1)S(1)} %collective-permute-done.105), channel_id=1, source_target_pairs={{0,8},{8,16},{16,24},{24,28},{28,20},{20,12},{12,4},{4,0},{1,9},{9... | collective-permute-start | bytes 786440 | tf_op jit(solution)/shard_map/ppermute | solution.py:382
  998.3 62.2 %collective-permute-start.19 = (f32[256,1024]{1,0:T(8,128)}, f32[256,1024]{1,0:T(8,128)S(1)}, u32[]{:S(2)}, u32[]{:S(2)}) collective-permute-start(f32[256,1024]{1,0:T(8,128)} %slice_select_fusion), channel_id=1, source_target_pairs={{0,2},{2,0},{1,3},{3,1},{4,6},{6,4},{5,7},{7,5},{8,10},{10,8},{9,1... | collective-permute-start | bytes 3145736 | tf_op jit(solution)/shard_map/ppermute | solution.py:345
  999.7 50.7 %collective-permute-start.62 = (bf16[64,4112]{1,0:T(8,128)(2,1)}, bf16[64,4112]{1,0:T(8,128)(2,1)S(1)}, u32[]{:S(2)}, u32[]{:S(2)}) collective-permute-start(bf16[64,4112]{1,0:T(8,128)(2,1)} %get-tuple-element.100), channel_id=1, source_target_pairs={{8,0},{16,8},{24,16},{28,24},{20,28},{12,20},{4,12},{0,4},{9,1},{1... | collective-permute-start | bytes 1579016 | tf_op jit(solution)/shard_map/ppermute | solution.py:366
  1009.7 40.7 %collective-permute-start.55 = (bf16[64,4112]{1,0:T(8,128)(2,1)S(1)}, bf16[64,4112]{1,0:T(8,128)(2,1)S(1)}, u32[]{:S(2)}, u32[]{:S(2)}) collective-permute-start(bf16[64,4112]{1,0:T(8,128)(2,1)S(1)} %get-tuple-element.101), channel_id=1, source_target_pairs={{0,8},{8,16},{16,24},{24,28},{28,20},{20,12},{12,4},{4,0},{1,9},{9... | collective-permute-start | bytes 1579016 | tf_op jit(solution)/shard_map/ppermute | solution.py:366
  1052.9 26.0 %collective-permute-start.63 = (bf16[64,4112]{1,0:T(8,128)(2,1)}, bf16[64,4112]{1,0:T(8,128)(2,1)S(1)}, u32[]{:S(2)}, u32[]{:S(2)}) collective-permute-start(bf16[64,4112]{1,0:T(8,128)(2,1)} %get-tuple-element.98), channel_id=1, source_target_pairs={{8,0},{16,8},{24,16},{28,24},{20,28},{12,20},{4,12},{0,4},{9,1},{1... | collective-permute-start | bytes 1579016 | tf_op jit(solution)/shard_map/ppermute | solution.py:366
  1052.9 26.0 %collective-permute-start.56 = (bf16[64,4112]{1,0:T(8,128)(2,1)}, bf16[64,4112]{1,0:T(8,128)(2,1)}, u32[]{:S(2)}, u32[]{:S(2)}) collective-permute-start(bf16[64,4112]{1,0:T(8,128)(2,1)} %get-tuple-element.99), channel_id=1, source_target_pairs={{0,8},{8,16},{16,24},{24,28},{28,20},{20,12},{12,4},{4,0},{1,9},{9... | collective-permute-start | bytes 1579016 | tf_op jit(solution)/shard_map/ppermute | solution.py:366
  1055.2 31.8 %collective-permute-start.43 = (bf16[64,2048]{1,0:T(8,128)(2,1)S(1)}, bf16[64,2048]{1,0:T(8,128)(2,1)}, u32[]{:S(2)}, u32[]{:S(2)}) collective-permute-start(bf16[64,2048]{1,0:T(8,128)(2,1)S(1)} %collective-permute-done.41), channel_id=1, source_target_pairs={{0,8},{8,16},{16,24},{24,28},{28,20},{20,12},{12,4},{4,0},{1,9},{9... | collective-permute-start | bytes 786440 | tf_op jit(solution)/shard_map/ppermute | solution.py:382
  1059.7 30.0 %collective-permute-start.44 = (bf16[64,2048]{1,0:T(8,128)(2,1)}, bf16[64,2048]{1,0:T(8,128)(2,1)}, u32[]{:S(2)}, u32[]{:S(2)}) collective-permute-start(bf16[64,2048]{1,0:T(8,128)(2,1)} %collective-permute-done.42), channel_id=1, source_target_pairs={{8,0},{16,8},{24,16},{28,24},{20,28},{12,20},{4,12},{0,4},{9,1},{1... | collective-permute-start | bytes 786440 | tf_op jit(solution)/shard_map/ppermute | solution.py:383
  1080.5 21.3 %collective-permute-start.64 = (bf16[64,4112]{1,0:T(8,128)(2,1)S(1)}, bf16[64,4112]{1,0:T(8,128)(2,1)S(1)}, u32[]{:S(2)}, u32[]{:S(2)}) collective-permute-start(bf16[64,4112]{1,0:T(8,128)(2,1)S(1)} %get-tuple-element.96), channel_id=1, source_target_pairs={{8,0},{16,8},{24,16},{28,24},{20,28},{12,20},{4,12},{0,4},{9,1},{1... | collective-permute-start | bytes 1579016 | tf_op jit(solution)/shard_map/ppermute | solution.py:366
  1132.1 27.9 %collective-permute-start.53 = (bf16[64,2048]{1,0:T(8,128)(2,1)S(1)}, bf16[64,2048]{1,0:T(8,128)(2,1)S(1)}, u32[]{:S(2)}, u32[]{:S(2)}) collective-permute-start(bf16[64,2048]{1,0:T(8,128)(2,1)S(1)} %collective-permute-done.51), channel_id=1, source_target_pairs={{0,8},{8,16},{16,24},{24,28},{28,20},{20,12},{12,4},{4,0},{1,9},{9... | collective-permute-start | bytes 786440 | tf_op jit(solution)/shard_map/ppermute | solution.py:382
  (204 other events, 3273.4 us)
